TPU v7x, 128 devices: a whole 4x4x4 slice. The times are simulated.
128 devices in a mesh: dp: 2 (over core), expert: 64 (over y, x, z).
Axes of the slice: x: 4, y: 4, z: 4, core: 2. Of those that a mesh axis runs over, the one named last changes fastest.
Arguments:
- tokens: bfloat16 [16384, 2048], P(('dp', 'expert')), may hold values from -6 to 6
- expert_ids: int32 [16384, 4], P(('dp', 'expert')), may hold values from 0 to 63, all different within a row; in each aligned block of 128 rows (0 to 127, 128 to 255, ...) at most 12 rows name the same one
- gate_weights: float32 [16384, 4], P(('dp', 'expert')), may hold values from 0.2 to 1
- w_gate: bfloat16 [64, 2048, 768], P('expert'), may hold values from -0.125 to 0.125
- w_up: bfloat16 [64, 2048, 768], P('expert'), may hold values from -0.125 to 0.125
- w_down: bfloat16 [64, 768, 2048], P('expert'), may hold values from -0.21875 to 0.21875
- out_grad: bfloat16 [16384, 2048], P(('dp', 'expert')), may hold values from -6 to 6
Outputs:
- mixed: bfloat16 [16384, 2048], P(('dp', 'expert'))
- grad_tokens: bfloat16 [16384, 2048], P(('dp', 'expert'))
- grad_gate: bfloat16 [64, 2048, 768], P('expert')
- grad_up: bfloat16 [64, 2048, 768], P('expert')
- grad_down: bfloat16 [64, 768, 2048], P('expert')
Inputs may be any that keep to these rules, and one draw needn't show every extreme that they name: `expert_ids`: each row names 4 different experts. Within the 128 rows of one device no expert is named by more than 12 rows, and in every draw some expert is named by exactly 12 rows of some device.
All inputs are finite; a program needn't handle non-finite values.
Results may differ from a plain program's by a relative error of at most 0.0066.
Values may be sent and summed in bfloat16 or wider, within the bound.
No kernel may reach another device: no remote copies, remote signals or barrier semaphores. Data moves between devices by JAX's collectives and lax.ppermute only.
A program may use at most 128 MiB of HBM per device.

v0:
```python
import jax
import jax.numpy as jnp
from jax import lax
from jax.experimental import pallas as pl
from jax.experimental.pallas import tpu as pltpu
from jax.sharding import PartitionSpec as P

F32 = jnp.float32
BF16 = jnp.bfloat16
FULL = 8
PART = 4
NO_SLOT = 99.0


def dot(left, right):
    return jnp.dot(left, right, preferred_element_type=F32)


def contract_rows(left, right):
    return lax.dot_general(left, right, (((1,), (1,)), ((), ())), preferred_element_type=F32)


def contract_cols(left, right):
    return lax.dot_general(left, right, (((0,), (0,)), ((), ())), preferred_element_type=F32)


def iota(shape, dim):
    return lax.broadcasted_iota(jnp.int32, shape, dim)


def dispatch_body(experts, ids_ref, gates_ref, tokens_ref, grad_ref, first_ref, second_ref, both_ref, sems):
    rows = tokens_ref.shape[0]

    @pl.when(pl.program_id(0) == 0)
    def _():
        copies = [
            pltpu.make_async_copy(tokens_ref, both_ref.at[pl.ds(0, rows)], sems.at[0]),
            pltpu.make_async_copy(grad_ref, both_ref.at[pl.ds(rows, rows)], sems.at[1]),
        ]
        for copy in copies:
            copy.start()
        for copy in copies:
            copy.wait()

    expert = iota((experts, rows), 0) + pl.program_id(0) * experts
    member = jnp.zeros((experts, rows), F32)
    gate = jnp.zeros((experts, rows), F32)
    for k in range(ids_ref.shape[0]):
        hit = ids_ref[k : k + 1, :] == expert
        member = jnp.where(hit, 1.0, member)
        gate = jnp.where(hit, gates_ref[k : k + 1, :], gate)
    earlier = jnp.where(iota((rows, rows), 0) < iota((rows, rows), 1), 1.0, 0.0).astype(BF16)
    rank = jnp.where(member > 0.5, dot(member.astype(BF16), earlier), NO_SLOT)

    def fill(out_ref, depth, base):
        shape = (experts, 2 * depth, rows)
        flat = (experts * 2 * depth, rows)
        row = iota(shape, 1)
        slot = (jnp.where(row < depth, row, row - depth) + base).astype(F32)
        is_token = row < depth
        hit = rank[:, None, :] == slot
        one = jnp.where(hit, 1.0, 0.0)
        of_token = jnp.where(is_token, one, 0.0).reshape(flat)
        of_grad = jnp.where(is_token, 0.0, one).reshape(flat)
        scale = jnp.where(hit, jnp.broadcast_to(gate[:, None, :], shape), 0.0)
        scale = jnp.sum(jnp.where(is_token, one, scale).reshape(flat), axis=1, keepdims=True)
        pick = jnp.concatenate([of_token, of_grad], axis=1).astype(BF16)
        out_ref[...] = (dot(pick, both_ref[...]) * scale).astype(BF16)

    fill(first_ref, FULL, 0)
    fill(second_ref, PART, FULL)


def dispatch(ids_t, gates_t, tokens, out_grad, experts, per_step):
    rows, width = tokens.shape
    top = ids_t.shape[0]
    whole = lambda shape: pl.BlockSpec(shape, lambda i: (0, 0))
    return pl.pallas_call(
        lambda *refs: dispatch_body(per_step, *refs),
        grid=(experts // per_step,),
        in_specs=[
            whole((top, rows)),
            whole((top, rows)),
            pl.BlockSpec(memory_space=pl.ANY),
            pl.BlockSpec(memory_space=pl.ANY),
        ],
        out_specs=[
            pl.BlockSpec((per_step * 2 * FULL, width), lambda i: (i, 0)),
            pl.BlockSpec((per_step * 2 * PART, width), lambda i: (i, 0)),
        ],
        out_shape=[
            jax.ShapeDtypeStruct((experts * 2 * FULL, width), BF16),
            jax.ShapeDtypeStruct((experts * 2 * PART, width), BF16),
        ],
        scratch_shapes=[pltpu.VMEM((2 * rows, width), BF16), pltpu.SemaphoreType.DMA((2,))],
        name="dispatch",
    )(ids_t, gates_t, tokens, out_grad)


def picker_body(experts, depth, ids_ref, gates_ref, pick_ref):
    rows, top = ids_ref.shape
    expert = iota((rows, experts), 1)
    member = jnp.zeros((rows, experts), F32)
    gate = jnp.zeros((rows, experts), F32)
    for k in range(top):
        hit = ids_ref[:, k : k + 1] == expert
        member = jnp.where(hit, 1.0, member)
        gate = jnp.where(hit, gates_ref[:, k : k + 1], gate)
    later = jnp.where(iota((rows, rows), 1) < iota((rows, rows), 0), 1.0, 0.0).astype(BF16)
    rank = jnp.where(member > 0.5, dot(later, member.astype(BF16)), NO_SLOT)
    high = gate.astype(BF16)
    low = (gate - high.astype(F32)).astype(BF16)
    total = experts * 2 * depth
    lane = iota((experts, total), 1) // (2 * depth)
    spread = jnp.where(lane == iota((experts, total), 0), 1.0, 0.0).astype(BF16)
    place = iota((rows, total), 1) % (2 * depth)
    slot = jnp.where(place < depth, place, jnp.where(place < FULL + 2 * PART, place - PART, place - FULL - 2 * PART))
    hit = dot(rank.astype(BF16), spread) == slot.astype(F32)
    back = hit & (place < depth)
    pick_ref[0:rows, :] = jnp.where(back, dot(high, spread), 0.0).astype(BF16)
    pick_ref[rows : 2 * rows, :] = jnp.where(back, dot(low, spread), 0.0).astype(BF16)
    pick_ref[2 * rows : 3 * rows, :] = jnp.where(hit & (place >= depth), 1.0, 0.0).astype(BF16)


def picker(ids, gates, experts):
    rows = ids.shape[0]
    depth = FULL + PART
    return pl.pallas_call(
        lambda *refs: picker_body(experts, depth, *refs),
        out_shape=jax.ShapeDtypeStruct((3 * rows, experts * 2 * depth), BF16),
        name="picker",
    )(ids, gates)


def combine_body(pick_ref, back_ref, mixed_ref, grad_ref):
    rows = mixed_ref.shape[0]
    total = dot(pick_ref[...], back_ref[...])
    mixed_ref[...] = (total[0:rows] + total[rows : 2 * rows]).astype(BF16)
    grad_ref[...] = total[2 * rows : 3 * rows].astype(BF16)


def combine(pick, back, rows, cols):
    total, width = back.shape
    out = jax.ShapeDtypeStruct((rows, width), BF16)
    return pl.pallas_call(
        combine_body,
        grid=(width // cols,),
        in_specs=[
            pl.BlockSpec((3 * rows, total), lambda i: (0, 0)),
            pl.BlockSpec((total, cols), lambda i: (0, i)),
        ],
        out_specs=[pl.BlockSpec((rows, cols), lambda i: (0, i))] * 2,
        out_shape=[out, out],
        name="combine",
    )(pick, back)


def expert_rows(x, cot, wg_ref, wu_ref, wd_ref):
    pre_gate = dot(x, wg_ref[...])
    pre_up = dot(x, wu_ref[...])
    sig = jax.nn.sigmoid(pre_gate)
    hidden = (pre_gate * sig * pre_up).astype(BF16)
    result = dot(hidden, wd_ref[...]).astype(BF16)
    d_hidden = contract_rows(cot, wd_ref[...])
    d_gate = (d_hidden * pre_up * sig * (1.0 + pre_gate * (1.0 - sig))).astype(BF16)
    d_up = (d_hidden * pre_gate * sig).astype(BF16)
    d_rows = (contract_rows(d_gate, wg_ref[...]) + contract_rows(d_up, wu_ref[...])).astype(BF16)
    return hidden, result, d_gate, d_up, d_rows


def main_body(tok_ref, cot_ref, wg_ref, wu_ref, wd_ref, back_ref, hid_ref, dg_ref, du_ref, res_buf, row_buf, sems):
    group, depth, width = tok_ref.shape
    step = pl.program_id(0)
    slot = step % 2

    def copies(at, buf):
        rows = pl.ds(at * group, group)
        return (
            pltpu.make_async_copy(res_buf.at[buf], back_ref.at[rows, pl.ds(0, FULL)], sems.at[0, buf]),
            pltpu.make_async_copy(row_buf.at[buf], back_ref.at[rows, pl.ds(FULL + 2 * PART, FULL)], sems.at[1, buf]),
        )

    @pl.when(step >= 2)
    def _():
        for copy in copies(step - 2, slot):
            copy.wait()

    flat = (group * depth, width)
    hidden, result, d_gate, d_up, d_rows = expert_rows(
        tok_ref[...].reshape(flat), cot_ref[...].reshape(flat), wg_ref, wu_ref, wd_ref
    )
    hid_ref[...] = hidden
    dg_ref[...] = d_gate
    du_ref[...] = d_up
    res_buf[slot] = result.reshape(group, depth, width)
    row_buf[slot] = d_rows.reshape(group, depth, width)
    for copy in copies(step, slot):
        copy.start()

    @pl.when(step == pl.num_programs(0) - 1)
    def _():
        @pl.when(step >= 1)
        def _():
            for copy in copies(step - 1, 1 - slot):
                copy.wait()

        for copy in copies(step, slot):
            copy.wait()


def main_experts(first, wg, wu, wd, group):
    sources, _, width = first.shape
    hidden_width = wg.shape[1]
    rows = sources * FULL
    small = jax.ShapeDtypeStruct((rows, hidden_width), BF16)
    fixed = lambda w: pl.BlockSpec(w.shape, lambda i: (0, 0), pipeline_mode=pl.Buffered(1))
    return pl.pallas_call(
        main_body,
        grid=(sources // group,),
        in_specs=[
            pl.BlockSpec((group, FULL, width), lambda i: (i, 0, 0)),
            pl.BlockSpec((group, FULL, width), lambda i: (i, 1, 0)),
            fixed(wg),
            fixed(wu),
            fixed(wd),
        ],
        out_specs=[pl.BlockSpec(memory_space=pl.ANY)]
        + [pl.BlockSpec((group * FULL, hidden_width), lambda i: (i, 0))] * 3,
        out_shape=[jax.ShapeDtypeStruct((sources, 2 * (FULL + PART), width), BF16), small, small, small],
        scratch_shapes=[
            pltpu.VMEM((2, group, FULL, width), BF16),
            pltpu.VMEM((2, group, FULL, width), BF16),
            pltpu.SemaphoreType.DMA((2, 2)),
        ],
        name="experts_main",
    )(first, first, wg, wu, wd)


def rest_body(mix_ref, wg_ref, wu_ref, wd_ref, old_ref, back_ref, tok_ref, cot_ref, hid_ref, dg_ref, du_ref, buf, sem):
    sources, depth, width = mix_ref.shape
    block = 256
    half = block // 2
    row = iota((block, block), 0)
    col = iota((block, block), 1)
    local = jnp.where(row < half, row, row - half)
    start = (local // PART) * (2 * PART) + local % PART + jnp.where(row < half, 0, PART)
    apart = jnp.where(col == start, 1.0, 0.0).astype(BF16)
    mix = mix_ref[...].reshape(sources * depth, width)
    n_blocks = sources * depth // block
    toks, cots = [], []
    for b in range(n_blocks):
        parts = dot(apart, mix[b * block : (b + 1) * block]).astype(BF16)
        toks.append(parts[:half])
        cots.append(parts[half:])
    tok = jnp.concatenate(toks, axis=0)
    cot = jnp.concatenate(cots, axis=0)
    hidden, result, d_gate, d_up, d_rows = expert_rows(tok, cot, wg_ref, wu_ref, wd_ref)
    for b in range(n_blocks):
        both = jnp.concatenate([result[b * half : (b + 1) * half], d_rows[b * half : (b + 1) * half]], axis=0)
        part = contract_cols(apart, both).astype(BF16)
        per = block // depth
        buf[b * per : (b + 1) * per] = part.reshape(per, depth, width)
    copy = pltpu.make_async_copy(buf, back_ref.at[:, pl.ds(FULL, 2 * PART)], sem)
    copy.start()
    tok_ref[...] = tok
    cot_ref[...] = cot
    hid_ref[...] = hidden
    dg_ref[...] = d_gate
    du_ref[...] = d_up
    copy.wait()


def rest_experts(second, wg, wu, wd, back):
    sources, depth, width = second.shape
    rows = sources * PART
    hidden_width = wg.shape[1]
    wide = jax.ShapeDtypeStruct((rows, width), BF16)
    small = jax.ShapeDtypeStruct((rows, hidden_width), BF16)
    vmem = pl.BlockSpec(memory_space=pltpu.VMEM)
    return pl.pallas_call(
        rest_body,
        in_specs=[vmem] * 4 + [pl.BlockSpec(memory_space=pl.ANY)],
        out_specs=[pl.BlockSpec(memory_space=pl.ANY)] + [vmem] * 5,
        out_shape=[jax.ShapeDtypeStruct(back.shape, BF16), wide, wide, small, small, small],
        input_output_aliases={4: 0},
        scratch_shapes=[pltpu.VMEM((sources, depth, width), BF16), pltpu.SemaphoreType.DMA(())],
        name="experts_rest",
    )(second, wg, wu, wd, back)


def exchange(blocks):
    return lax.all_to_all(blocks, "expert", split_axis=0, concat_axis=0, tiled=True)


def replica_sum(part):
    other = lax.ppermute(part, "dp", [(0, 1), (1, 0)])
    return (part.astype(F32) + other.astype(F32)).astype(BF16)


def on_device(tokens, expert_ids, gate_weights, w_gate, w_up, w_down, out_grad):
    experts = lax.axis_size("expert")
    rows, width = tokens.shape
    wg, wu, wd = w_gate[0], w_up[0], w_down[0]
    first, second = dispatch(expert_ids.T, gate_weights.T, tokens, out_grad, experts, 8)
    first = exchange(first.reshape(experts, 2 * FULL, width))
    second = exchange(second.reshape(experts, 2 * PART, width))
    pick = picker(expert_ids, gate_weights, experts)
    back, hid_a, dg_a, du_a = main_experts(first, wg, wu, wd, 32)
    back, tok_b, cot_b, hid_b, dg_b, du_b = rest_experts(second, wg, wu, wd, back)
    back = exchange(back).reshape(-1, width)
    tok = jnp.concatenate([first[:, :FULL].reshape(-1, width), tok_b], axis=0)
    cot = jnp.concatenate([first[:, FULL:].reshape(-1, width), cot_b], axis=0)
    hid = jnp.concatenate([hid_a, hid_b], axis=0)
    d_gate = jnp.concatenate([dg_a, dg_b], axis=0)
    d_up = jnp.concatenate([du_a, du_b], axis=0)
    grad_gate = replica_sum(contract_cols(tok, d_gate).astype(BF16))
    grad_up = replica_sum(contract_cols(tok, d_up).astype(BF16))
    grad_down = replica_sum(contract_cols(hid, cot).astype(BF16))
    mixed, grad_tokens = combine(pick, back, rows, 512)
    return mixed, grad_tokens, grad_gate[None], grad_up[None], grad_down[None]


def solution(mesh):
    by_row = P(("dp", "expert"), None)
    by_expert = P("expert", None, None)
    return jax.shard_map(
        on_device,
        mesh=mesh,
        in_specs=(by_row, by_row, by_row, by_expert, by_expert, by_expert, by_row),
        out_specs=(by_row, by_row, by_expert, by_expert, by_expert),
        check_vma=False,
    )
```

profile of v0, /device:TPU:4, one launch (start us, length us, event | category | flops | bytes accessed | tf_op | source)
XLA Modules:
  0.0 218.2 jit_solution(8602070035128797939)
XLA Ops:
  0.6 7.8 %dispatch.1 = (bf16[1024,2048]{1,0:T(8,128)(2,1)}, bf16[512,2048]{1,0:T(8,128)(2,1)}) custom-call(s32[4,128]{1,0:T(4,128)} %bitcast.26, f32[4,128]{1,0:T(4,128)} %bitcast.27, bf16[128,2048]{1,0:T(8,128)(2,1)} %refs_2_.1, bf16[128,2048]{1,0:T(8,128)(2,1)} %refs_3_.1), custom_call_target="tpu_custom_call" | custom-call | tf_op jit(solution)/shard_map/dispatch/pallas_call | solution.py:78
  8.4 61.4 %all_to_all.15.tok_ref.cot_ref = bf16[64,16,2048]{2,1,0:T(8,128)(2,1)} all-to-all(bf16[64,16,2048]{2,1,0:T(8,128)(2,1)} %bitcast.24), channel_id=1, replica_groups=mesh['dp'=2,'expert'=64] {'expert'}, dimensions={0} | all-to-all | bytes 8388608 | tf_op jit(solution)/shard_map/all_to_all | solution.py:292
  69.9 7.8 %all-to-all-start = ((bf16[64,8,2048]{2,1,0:T(8,128)(2,1)}), bf16[64,8,2048]{2,1,0:T(8,128)(2,1)S(1)}, u32[]{:S(2)}, u32[]{:S(2)}) async-start(bf16[64,8,2048]{2,1,0:T(8,128)(2,1)} %bitcast.25), calls=%async_computation | async-start | bytes 4194304 | tf_op jit(solution)/shard_map/all_to_all | solution.py:292
  77.7 18.3 %experts_main.1 = (bf16[64,24,2048]{2,1,0:T(8,128)(2,1)}, bf16[512,768]{1,0:T(8,128)(2,1)}, bf16[512,768]{1,0:T(8,128)(2,1)}, bf16[512,768]{1,0:T(8,128)(2,1)}) custom-call(bf16[64,16,2048]{2,1,0:T(8,128)(2,1)} %all_to_all.15.tok_ref.cot_ref, bf16[64,16,2048]{2,1,0:T(8,128)(2,1)} %all_to_all.15.tok_ref.cot_ref, bf16[2048,768]{1,0:T(8,128)(2,1)} %bitcast.18, ...), custom_call_target="tpu_custom_call" | custom-call | tf_op jit(solution)/shard_map/experts_main/pallas_call | solution.py:217
  96.0 7.4 %all-to-all-done.mix_ref = bf16[64,8,2048]{2,1,0:T(8,128)(2,1)S(1)} async-done(((bf16[64,8,2048]{2,1,0:T(8,128)(2,1)}), bf16[64,8,2048]{2,1,0:T(8,128)(2,1)S(1)}, u32[]{:S(2)}, u32[]{:S(2)}) %all-to-all-start) | async-done | bytes 2097184 | tf_op jit(solution)/shard_map/all_to_all | solution.py:292
  103.5 0.0 copy-start
  103.5 1.3 copy-done
  104.8 14.3 %experts_rest.1 = (bf16[64,24,2048]{2,1,0:T(8,128)(2,1)}, bf16[256,2048]{1,0:T(8,128)(2,1)}, bf16[256,2048]{1,0:T(8,128)(2,1)}, bf16[256,768]{1,0:T(8,128)(2,1)}...) custom-call(bf16[64,8,2048]{2,1,0:T(8,128)(2,1)} %copy-done, ...), custom_call_target="tpu_custom_call", output_to_operand_aliasing={{0}: (4, {})} | custom-call | tf_op jit(solution)/shard_map/experts_rest/pallas_call | solution.py:280
  119.1 8.0 %all-to-all-start.2 = ((bf16[64,24,2048]{2,1,0:T(8,128)(2,1)}), bf16[64,24,2048]{2,1,0:T(8,128)(2,1)}, u32[]{:S(2)}, u32[]{:S(2)}) async-start(bf16[64,24,2048]{2,1,0:T(8,128)(2,1)} %get-tuple-element.22), calls=%async_computation.2 | async-start | bytes 12582912 | tf_op jit(solution)/shard_map/all_to_all | solution.py:292
  127.1 0.0 copy-start.4
  127.1 0.0 copy-start.7
  127.1 0.0 copy-start.10
  127.1 2.9 %slice_bitcast_fusion = (bf16[512,2048]{1,0:T(8,128)(2,1)S(1)}, bf16[512,2048]{1,0:T(8,128)(2,1)S(1)}) fusion(bf16[64,16,2048]{2,1,0:T(8,128)(2,1)} %all_to_all.15.tok_ref.cot_ref), kind=kLoop, calls=%fused_computation.13 | loop fusion | bytes 8388608 | tf_op jit(solution)/shard_map/reshape | solution.py:312
  130.0 0.0 copy-done.4
  130.0 0.0 copy-done.7
  130.0 0.0 copy-done.10
  130.0 0.0 copy-start.3
  130.0 0.0 copy-start.6
  130.1 0.0 copy-start.9
  130.1 2.9 %convolution_convert_fusion = bf16[768,2048]{1,0:T(8,128)(2,1)S(1)} fusion(bf16[256,2048]{1,0:T(8,128)(2,1)S(1)} %copy-done.4, bf16[512,2048]{1,0:T(8,128)(2,1)S(1)} %get-tuple-element.33, bf16[256,768]{1,0:T(8,128)(2,1)S(1)} %copy-done.10, bf16[512,768]{1,0:T(8,128)(2,1)S(1)} %copy-done.7), kind=kOutput, calls=%fused_computation.3 | convolution fusion | flops 2426142720 | bytes 7471104 | tf_op jit(solution)/shard_map/dot_general | solution.py:24
  133.0 0.1 collective-permute-start.2
  133.1 0.0 copy-done.3
  133.1 0.0 copy-done.6
  133.1 0.0 copy-done.9
  133.1 0.0 copy-start.5
  133.1 0.0 copy-start.8
  133.1 4.1 %convolution_convert_fusion.1 = bf16[2048,768]{1,0:T(8,128)(2,1)} fusion(bf16[256,2048]{1,0:T(8,128)(2,1)S(1)} %copy-done.3, bf16[512,2048]{1,0:T(8,128)(2,1)S(1)} %get-tuple-element.34, bf16[256,768]{1,0:T(8,128)(2,1)S(1)} %copy-done.9, bf16[512,768]{1,0:T(8,128)(2,1)S(1)} %copy-done.6), kind=kOutput, calls=%fused_computation.4 | convolution fusion | flops 2426142720 | bytes 7471104 | tf_op jit(solution)/shard_map/dot_general | solution.py:24
  137.2 0.5 collective-permute-start.1
  137.6 0.0 copy-done.5
  137.6 0.0 copy-done.8
  137.7 0.0 copy-start.1
  137.7 0.0 copy-start.2
  137.7 4.1 %convolution_convert_fusion.2 = bf16[2048,768]{1,0:T(8,128)(2,1)} fusion(bf16[256,2048]{1,0:T(8,128)(2,1)S(1)} %copy-done.3, bf16[512,2048]{1,0:T(8,128)(2,1)S(1)} %get-tuple-element.34, bf16[256,768]{1,0:T(8,128)(2,1)S(1)} %copy-done.8, bf16[512,768]{1,0:T(8,128)(2,1)S(1)} %copy-done.5), kind=kOutput, calls=%fused_computation.5 | convolution fusion | flops 2426142720 | bytes 7471104 | tf_op jit(solution)/shard_map/dot_general | solution.py:24
  141.7 0.0 collective-permute-start
  141.8 0.0 copy-done.1
  141.8 0.7 copy.13.refs_0_
  142.5 0.0 copy-done.2
  142.5 0.7 copy.14.refs_1_
  143.3 2.7 %picker.1.pick_ref = bf16[384,1536]{1,0:T(8,128)(2,1)} custom-call(s32[128,4]{1,0:T(8,128)} %copy.13.refs_0_, f32[128,4]{1,0:T(8,128)} %copy.14.refs_1_), custom_call_target="tpu_custom_call" | custom-call | tf_op jit(solution)/shard_map/picker/pallas_call | solution.py:128
  146.0 0.0 collective-permute-done.2
  146.0 4.9 %fusion.2 = bf16[1,768,2048]{2,1,0:T(8,128)(2,1)} fusion(bf16[768,2048]{1,0:T(8,128)(2,1)} %collective-permute-done.2, bf16[768,2048]{1,0:T(8,128)(2,1)S(1)} %convolution_convert_fusion), kind=kLoop, calls=%fused_computation.8 | loop fusion | flops 6291456 | bytes 9437184 | tf_op jit(solution)/shard_map/broadcast_in_dim | solution.py:320
  150.8 0.0 collective-permute-done.1
  150.8 5.3 %fusion.1 = bf16[1,2048,768]{2,1,0:T(8,128)(2,1)} fusion(bf16[2048,768]{1,0:T(8,128)(2,1)} %collective-permute-done.1, bf16[2048,768]{1,0:T(8,128)(2,1)} %convolution_convert_fusion.1), kind=kLoop, calls=%fused_computation.7 | loop fusion | flops 6291456 | bytes 9437184 | tf_op jit(solution)/shard_map/broadcast_in_dim | solution.py:320
  156.1 0.0 collective-permute-done
  156.1 5.3 %fusion = bf16[1,2048,768]{2,1,0:T(8,128)(2,1)} fusion(bf16[2048,768]{1,0:T(8,128)(2,1)} %collective-permute-done, bf16[2048,768]{1,0:T(8,128)(2,1)} %convolution_convert_fusion.2), kind=kLoop, calls=%fused_computation.6 | loop fusion | flops 6291456 | bytes 9437184 | tf_op jit(solution)/shard_map/broadcast_in_dim | solution.py:320
  161.4 50.4 %all-to-all-done.2 = bf16[64,24,2048]{2,1,0:T(8,128)(2,1)} async-done(((bf16[64,24,2048]{2,1,0:T(8,128)(2,1)}), bf16[64,24,2048]{2,1,0:T(8,128)(2,1)}, u32[]{:S(2)}, u32[]{:S(2)}) %all-to-all-start.2) | async-done | bytes 6291488 | tf_op jit(solution)/shard_map/all_to_all | solution.py:292
  211.8 6.4 %combine.1 = (bf16[128,2048]{1,0:T(8,128)(2,1)}, bf16[128,2048]{1,0:T(8,128)(2,1)}) custom-call(bf16[384,1536]{1,0:T(8,128)(2,1)} %picker.1.pick_ref, bf16[1536,2048]{1,0:T(8,128)(2,1)} %bitcast.7.back_ref), custom_call_target="tpu_custom_call" | custom-call | tf_op jit(solution)/shard_map/combine/pallas_call | solution.py:145
Async XLA Ops:
  69.9 33.6 %all-to-all-start = ((bf16[64,8,2048]{2,1,0:T(8,128)(2,1)}), bf16[64,8,2048]{2,1,0:T(8,128)(2,1)S(1)}, u32[]{:S(2)}, u32[]{:S(2)}) async-start(bf16[64,8,2048]{2,1,0:T(8,128)(2,1)} %bitcast.25), calls=%async_computation | async-start | bytes 4194304 | tf_op jit(solution)/shard_map/all_to_all | solution.py:292
  103.5 1.3 copy-start
  119.1 92.7 %all-to-all-start.2 = ((bf16[64,24,2048]{2,1,0:T(8,128)(2,1)}), bf16[64,24,2048]{2,1,0:T(8,128)(2,1)}, u32[]{:S(2)}, u32[]{:S(2)}) async-start(bf16[64,24,2048]{2,1,0:T(8,128)(2,1)} %get-tuple-element.22), calls=%async_computation.2 | async-start | bytes 12582912 | tf_op jit(solution)/shard_map/all_to_all | solution.py:292
  127.1 2.9 %copy-start.4 = (bf16[256,2048]{1,0:T(8,128)(2,1)S(1)}, bf16[256,2048]{1,0:T(8,128)(2,1)}, u32[]{:S(2)}) copy-start(bf16[256,2048]{1,0:T(8,128)(2,1)} %get-tuple-element.32) | copy-start | bytes 3145732
  127.1 2.9 %copy-start.7 = (bf16[512,768]{1,0:T(8,128)(2,1)S(1)}, bf16[512,768]{1,0:T(8,128)(2,1)}, u32[]{:S(2)}) copy-start(bf16[512,768]{1,0:T(8,128)(2,1)} %get-tuple-element.30) | copy-start | bytes 2359300
  127.1 2.9 %copy-start.10 = (bf16[256,768]{1,0:T(8,128)(2,1)S(1)}, bf16[256,768]{1,0:T(8,128)(2,1)}, u32[]{:S(2)}) copy-start(bf16[256,768]{1,0:T(8,128)(2,1)} %get-tuple-element.31) | copy-start | bytes 1179652
  130.0 3.0 %copy-start.3 = (bf16[256,2048]{1,0:T(8,128)(2,1)S(1)}, bf16[256,2048]{1,0:T(8,128)(2,1)}, u32[]{:S(2)}) copy-start(bf16[256,2048]{1,0:T(8,128)(2,1)} %get-tuple-element.25) | copy-start | bytes 3145732
  130.0 3.0 %copy-start.6 = (bf16[512,768]{1,0:T(8,128)(2,1)S(1)}, bf16[512,768]{1,0:T(8,128)(2,1)}, u32[]{:S(2)}) copy-start(bf16[512,768]{1,0:T(8,128)(2,1)} %get-tuple-element.28) | copy-start | bytes 2359300
  130.1 3.0 %copy-start.9 = (bf16[256,768]{1,0:T(8,128)(2,1)S(1)}, bf16[256,768]{1,0:T(8,128)(2,1)}, u32[]{:S(2)}) copy-start(bf16[256,768]{1,0:T(8,128)(2,1)} %get-tuple-element.29) | copy-start | bytes 1179652
  133.0 13.0 %collective-permute-start.2 = (bf16[768,2048]{1,0:T(8,128)(2,1)S(1)}, bf16[768,2048]{1,0:T(8,128)(2,1)}, u32[]{:S(2)}, u32[]{:S(2)}) collective-permute-start(bf16[768,2048]{1,0:T(8,128)(2,1)S(1)} %convolution_convert_fusion), channel_id=1, source_target_pairs={{0,64},{64,0},{1,65},{65,1},{2,66},{66,2},{3,67},{67,3},{4,68},{68... | collective-permute-start | bytes 9437192 | tf_op jit(solution)/shard_map/ppermute | solution.py:296
  133.1 4.6 %copy-start.5 = (bf16[512,768]{1,0:T(8,128)(2,1)S(1)}, bf16[512,768]{1,0:T(8,128)(2,1)}, u32[]{:S(2)}) copy-start(bf16[512,768]{1,0:T(8,128)(2,1)} %get-tuple-element.26) | copy-start | bytes 2359300
  133.1 4.6 %copy-start.8 = (bf16[256,768]{1,0:T(8,128)(2,1)S(1)}, bf16[256,768]{1,0:T(8,128)(2,1)}, u32[]{:S(2)}) copy-start(bf16[256,768]{1,0:T(8,128)(2,1)} %get-tuple-element.27) | copy-start | bytes 1179652
  137.2 13.7 %collective-permute-start.1 = (bf16[2048,768]{1,0:T(8,128)(2,1)}, bf16[2048,768]{1,0:T(8,128)(2,1)}, u32[]{:S(2)}, u32[]{:S(2)}) collective-permute-start(bf16[2048,768]{1,0:T(8,128)(2,1)} %convolution_convert_fusion.1), channel_id=1, source_target_pairs={{0,64},{64,0},{1,65},{65,1},{2,66},{66,2},{3,67},{67,3},{4,68},{68... | collective-permute-start | bytes 9437192 | tf_op jit(solution)/shard_map/ppermute | solution.py:296
  137.7 4.1 %copy-start.1 = (s32[128,4]{0,1:T(4,128)S(1)}, s32[128,4]{0,1:T(4,128)}, u32[]{:S(2)}) copy-start(s32[128,4]{0,1:T(4,128)} %param.8) | copy-start | bytes 6148
  137.7 4.9 %copy-start.2 = (f32[128,4]{0,1:T(4,128)S(1)}, f32[128,4]{0,1:T(4,128)}, u32[]{:S(2)}) copy-start(f32[128,4]{0,1:T(4,128)} %param.9) | copy-start | bytes 6148
  141.7 14.4 %collective-permute-start = (bf16[2048,768]{1,0:T(8,128)(2,1)}, bf16[2048,768]{1,0:T(8,128)(2,1)}, u32[]{:S(2)}, u32[]{:S(2)}) collective-permute-start(bf16[2048,768]{1,0:T(8,128)(2,1)} %convolution_convert_fusion.2), channel_id=1, source_target_pairs={{0,64},{64,0},{1,65},{65,1},{2,66},{66,2},{3,67},{67,3},{4,68},{68... | collective-permute-start | bytes 9437192 | tf_op jit(solution)/shard_map/ppermute | solution.py:296
where the time goes:
time: 219 us; the launch traced here: 218 us
  blocking collectives  61.4 us (28%)
  waiting for transfers between devices  57.8 us (26%)
  Pallas kernels  49.5 us (23%)
  starting transfers between devices  16.4 us (7%)
  other arithmetic  15.5 us (7%)
  matrix products  11 us (5%)
  local copies, waits for them, and re-layouts  5.73 us (3%)
    all_to_all x1, blocking collectives, exchange(): lax.all_to_all(blocks, 'expert', split_axis=0, concat_axis=0, tiled=True)  61.4 us
    all_to_all x2, waiting for transfers between devices, exchange(): lax.all_to_all(blocks, 'expert', split_axis=0, concat_axis=0, tiled=True)  57.8 us
    pallas_call x1, Pallas kernels, main_experts(): pl.pallas_call(main_body, grid=(sources // group,), in_specs=[pl.BlockSpe...  18.3 us
    all_to_all x2, starting transfers between devices, exchange(): lax.all_to_all(blocks, 'expert', split_axis=0, concat_axis=0, tiled=True)  15.8 us
    broadcast_in_dim x3, other arithmetic, on_device(): return (mixed, grad_tokens, grad_gate[None], grad_up[None], grad_down[None])  15.5 us
    pallas_call x1, Pallas kernels, rest_experts(): pl.pallas_call(rest_body, in_specs=[vmem] * 4 + [pl.BlockSpec(memory_spac...  14.3 us
    dot_general x3, matrix products, contract_cols(): lax.dot_general(left, right, (((0,), (0,)), ((), ())), preferred_element_...  11 us
    pallas_call x1, Pallas kernels, dispatch(): pl.pallas_call(lambda *refs: dispatch_body(per_step, *refs), grid=(expert...  7.8 us
  transfers between devices with their start and end apart: 5, of which 2 were waited for; matrix products, arithmetic and copies ran while one was open for 14% of the time, Pallas kernels for 10%

commit v1 on v0

v1 whole, which is shorter than its diff:
```python
import jax
import jax.numpy as jnp
from jax import lax
from jax.experimental import pallas as pl
from jax.experimental.pallas import tpu as pltpu
from jax.sharding import PartitionSpec as P


F32 = jnp.float32
BF16 = jnp.bfloat16
FULL = 8
PART = 4
NO_SLOT = 99.0


def dot(left, right):
    return jnp.dot(left, right, preferred_element_type=F32)


def contract_rows(left, right):
    return lax.dot_general(left, right, (((1,), (1,)), ((), ())), preferred_element_type=F32)


def contract_cols(left, right):
    return lax.dot_general(left, right, (((0,), (0,)), ((), ())), preferred_element_type=F32)


def iota(shape, dim):
    return lax.broadcasted_iota(jnp.int32, shape, dim)


def dispatch_body(experts, ids_ref, gates_ref, tokens_ref, grad_ref, first_ref, second_ref, both_ref, sems):
    rows = tokens_ref.shape[0]

    @pl.when(pl.program_id(0) == 0)
    def _():
        copies = [
            pltpu.make_async_copy(tokens_ref, both_ref.at[pl.ds(0, rows)], sems.at[0]),
            pltpu.make_async_copy(grad_ref, both_ref.at[pl.ds(rows, rows)], sems.at[1]),
        ]
        for copy in copies:
            copy.start()
        for copy in copies:
            copy.wait()

    expert = iota((experts, rows), 0) + pl.program_id(0) * experts
    member = jnp.zeros((experts, rows), F32)
    gate = jnp.zeros((experts, rows), F32)
    for k in range(ids_ref.shape[0]):
        hit = ids_ref[k : k + 1, :] == expert
        member = jnp.where(hit, 1.0, member)
        gate = jnp.where(hit, gates_ref[k : k + 1, :], gate)
    earlier = jnp.where(iota((rows, rows), 0) < iota((rows, rows), 1), 1.0, 0.0).astype(BF16)
    rank = jnp.where(member > 0.5, dot(member.astype(BF16), earlier), NO_SLOT)

    def fill(out_ref, depth, base):
        shape = (experts, 2 * depth, rows)
        flat = (experts * 2 * depth, rows)
        row = iota(shape, 1)
        slot = (jnp.where(row < depth, row, row - depth) + base).astype(F32)
        is_token = row < depth
        hit = rank[:, None, :] == slot
        one = jnp.where(hit, 1.0, 0.0)
        of_token = jnp.where(is_token, one, 0.0).reshape(flat)
        of_grad = jnp.where(is_token, 0.0, one).reshape(flat)
        scale = jnp.where(hit, jnp.broadcast_to(gate[:, None, :], shape), 0.0)
        scale = jnp.sum(jnp.where(is_token, one, scale).reshape(flat), axis=1, keepdims=True)
        pick = jnp.concatenate([of_token, of_grad], axis=1).astype(BF16)
        out_ref[...] = (dot(pick, both_ref[...]) * scale).astype(BF16)

    fill(first_ref, FULL, 0)
    fill(second_ref, PART, FULL)


def dispatch(ids_t, gates_t, tokens, out_grad, experts, per_step):
    rows, width = tokens.shape
    top = ids_t.shape[0]
    whole = lambda shape: pl.BlockSpec(shape, lambda i: (0, 0))
    return pl.pallas_call(
        lambda *refs: dispatch_body(per_step, *refs),
        grid=(experts // per_step,),
        in_specs=[
            whole((top, rows)),
            whole((top, rows)),
            pl.BlockSpec(memory_space=pl.ANY),
            pl.BlockSpec(memory_space=pl.ANY),
        ],
        out_specs=[
            pl.BlockSpec((per_step * 2 * FULL, width), lambda i: (i, 0)),
            pl.BlockSpec((per_step * 2 * PART, width), lambda i: (i, 0)),
        ],
        out_shape=[
            jax.ShapeDtypeStruct((experts * 2 * FULL, width), BF16),
            jax.ShapeDtypeStruct((experts * 2 * PART, width), BF16),
        ],
        scratch_shapes=[pltpu.VMEM((2 * rows, width), BF16), pltpu.SemaphoreType.DMA((2,))],
        name="dispatch",
    )(ids_t, gates_t, tokens, out_grad)


def picker_body(experts, ids_ref, gates_ref, full_ref, part_ref):
    rows, top = ids_ref.shape
    expert = iota((rows, experts), 1)
    member = jnp.zeros((rows, experts), F32)
    gate = jnp.zeros((rows, experts), F32)
    for k in range(top):
        hit = ids_ref[:, k : k + 1] == expert
        member = jnp.where(hit, 1.0, member)
        gate = jnp.where(hit, gates_ref[:, k : k + 1], gate)
    later = jnp.where(iota((rows, rows), 1) < iota((rows, rows), 0), 1.0, 0.0).astype(BF16)
    rank = jnp.where(member > 0.5, dot(later, member.astype(BF16)), NO_SLOT).astype(BF16)
    high = gate.astype(BF16)
    low = (gate - high.astype(F32)).astype(BF16)

    def fill(out_ref, depth, base):
        total = experts * 2 * depth
        spread = jnp.where(iota((experts, total), 1) // (2 * depth) == iota((experts, total), 0), 1.0, 0.0).astype(BF16)
        place = iota((rows, total), 1) % (2 * depth)
        slot = jnp.where(place < depth, place, place - depth) + base
        hit = dot(rank, spread) == slot.astype(F32)
        back = hit & (place < depth)
        out_ref[0:rows, :] = jnp.where(back, dot(high, spread), 0.0).astype(BF16)
        out_ref[rows : 2 * rows, :] = jnp.where(back, dot(low, spread), 0.0).astype(BF16)
        out_ref[2 * rows : 3 * rows, :] = jnp.where(hit & (place >= depth), 1.0, 0.0).astype(BF16)

    fill(full_ref, FULL, 0)
    fill(part_ref, PART, FULL)


def picker(ids, gates, experts):
    rows = ids.shape[0]
    return pl.pallas_call(
        lambda *refs: picker_body(experts, *refs),
        out_shape=[
            jax.ShapeDtypeStruct((3 * rows, experts * 2 * FULL), BF16),
            jax.ShapeDtypeStruct((3 * rows, experts * 2 * PART), BF16),
        ],
        name="picker",
    )(ids, gates)


def gather_body(pick_ref, back_ref, mixed_ref, grad_ref):
    rows = mixed_ref.shape[0]
    total = dot(pick_ref[...], back_ref[...])
    mixed_ref[...] = total[0:rows] + total[rows : 2 * rows]
    grad_ref[...] = total[2 * rows : 3 * rows]


def finish_body(pick_ref, back_ref, mixed_old_ref, grad_old_ref, mixed_ref, grad_ref):
    rows = mixed_ref.shape[0]
    total = dot(pick_ref[...], back_ref[...])
    mixed_ref[...] = (mixed_old_ref[...] + total[0:rows] + total[rows : 2 * rows]).astype(BF16)
    grad_ref[...] = (grad_old_ref[...] + total[2 * rows : 3 * rows]).astype(BF16)


def gather(pick, back, cols):
    rows = pick.shape[0] // 3
    total, width = back.shape
    out = jax.ShapeDtypeStruct((rows, width), F32)
    by_cols = lambda count: pl.BlockSpec((count, cols), lambda i: (0, i))
    return pl.pallas_call(
        gather_body,
        grid=(width // cols,),
        in_specs=[pl.BlockSpec(pick.shape, lambda i: (0, 0)), by_cols(total)],
        out_specs=[by_cols(rows)] * 2,
        out_shape=[out, out],
        name="gather",
    )(pick, back)


def finish(pick, back, old):
    out = jax.ShapeDtypeStruct(old[0].shape, BF16)
    return pl.pallas_call(
        finish_body,
        in_specs=[pl.BlockSpec(memory_space=pltpu.VMEM)] * 4,
        out_shape=[out, out],
        compiler_params=pltpu.CompilerParams(vmem_limit_bytes=24 << 20),
        name="finish",
    )(*map(in_vmem, (pick, back, *old)))


def in_vmem(array):
    return pltpu.with_memory_space_constraint(array, pltpu.VMEM)


def expert_rows(x, cot, wg_ref, wu_ref, wd_ref):
    pre_gate = dot(x, wg_ref[...])
    pre_up = dot(x, wu_ref[...])
    sig = jax.nn.sigmoid(pre_gate)
    hidden = (pre_gate * sig * pre_up).astype(BF16)
    result = dot(hidden, wd_ref[...]).astype(BF16)
    d_hidden = contract_rows(cot, wd_ref[...])
    d_gate = (d_hidden * pre_up * sig * (1.0 + pre_gate * (1.0 - sig))).astype(BF16)
    d_up = (d_hidden * pre_gate * sig).astype(BF16)
    d_rows = (contract_rows(d_gate, wg_ref[...]) + contract_rows(d_up, wu_ref[...])).astype(BF16)
    return hidden, result, d_gate, d_up, d_rows


def main_body(tok_ref, cot_ref, wg_ref, wu_ref, wd_ref, back_ref, hid_ref, dg_ref, du_ref):
    group, depth, width = tok_ref.shape
    flat = (group * depth, width)
    hidden, result, d_gate, d_up, d_rows = expert_rows(
        tok_ref[...].reshape(flat), cot_ref[...].reshape(flat), wg_ref, wu_ref, wd_ref
    )
    hid_ref[...] = hidden
    dg_ref[...] = d_gate
    du_ref[...] = d_up
    back_ref[:, 0:depth] = result.reshape(group, depth, width)
    back_ref[:, depth : 2 * depth] = d_rows.reshape(group, depth, width)


def main_experts(first, wg, wu, wd, group):
    sources, both, width = first.shape
    hidden_width = wg.shape[1]
    small = jax.ShapeDtypeStruct((sources * FULL, hidden_width), BF16)
    fixed = lambda w: pl.BlockSpec(w.shape, lambda i: (0, 0), pipeline_mode=pl.Buffered(1))
    return pl.pallas_call(
        main_body,
        grid=(sources // group,),
        in_specs=[
            pl.BlockSpec((group, FULL, width), lambda i: (i, 0, 0)),
            pl.BlockSpec((group, FULL, width), lambda i: (i, 1, 0)),
            fixed(wg),
            fixed(wu),
            fixed(wd),
        ],
        out_specs=[pl.BlockSpec((group, both, width), lambda i: (i, 0, 0))]
        + [pl.BlockSpec((group * FULL, hidden_width), lambda i: (i, 0))] * 3,
        out_shape=[jax.ShapeDtypeStruct(first.shape, BF16), small, small, small],
        name="experts_main",
    )(first, first, wg, wu, wd)


def rest_body(mix_ref, wg_ref, wu_ref, wd_ref, back_ref, tok_ref, cot_ref, hid_ref, dg_ref, du_ref):
    sources, depth, width = mix_ref.shape
    block = 256
    half = block // 2
    row = iota((block, block), 0)
    col = iota((block, block), 1)
    local = jnp.where(row < half, row, row - half)
    start = (local // PART) * (2 * PART) + local % PART + jnp.where(row < half, 0, PART)
    apart = jnp.where(col == start, 1.0, 0.0).astype(BF16)
    mix = mix_ref[...].reshape(sources * depth, width)
    n_blocks = sources * depth // block
    toks, cots = [], []
    for b in range(n_blocks):
        parts = dot(apart, mix[b * block : (b + 1) * block]).astype(BF16)
        toks.append(parts[:half])
        cots.append(parts[half:])
    tok = jnp.concatenate(toks, axis=0)
    cot = jnp.concatenate(cots, axis=0)
    hidden, result, d_gate, d_up, d_rows = expert_rows(tok, cot, wg_ref, wu_ref, wd_ref)
    per = block // depth
    for b in range(n_blocks):
        both = jnp.concatenate([result[b * half : (b + 1) * half], d_rows[b * half : (b + 1) * half]], axis=0)
        back_ref[b * per : (b + 1) * per] = contract_cols(apart, both).astype(BF16).reshape(per, depth, width)
    tok_ref[...] = tok
    cot_ref[...] = cot
    hid_ref[...] = hidden
    dg_ref[...] = d_gate
    du_ref[...] = d_up


def rest_experts(second, wg, wu, wd):
    sources, _, width = second.shape
    rows = sources * PART
    wide = jax.ShapeDtypeStruct((rows, width), BF16)
    small = jax.ShapeDtypeStruct((rows, wg.shape[1]), BF16)
    return pl.pallas_call(
        rest_body,
        in_specs=[pl.BlockSpec(memory_space=pltpu.VMEM)] * 4,
        out_shape=[jax.ShapeDtypeStruct(second.shape, BF16), wide, wide, small, small, small],
        compiler_params=pltpu.CompilerParams(vmem_limit_bytes=48 << 20),
        name="experts_rest",
    )(in_vmem(second), wg, wu, wd)


def exchange(blocks):
    return lax.all_to_all(blocks, "expert", split_axis=0, concat_axis=0, tiled=True)


def replica_sum(part):
    other = lax.ppermute(part, "dp", [(0, 1), (1, 0)])
    return (part.astype(F32) + other.astype(F32)).astype(BF16)


def layer(tokens, expert_ids, gate_weights, w_gate, w_up, w_down, out_grad):
    experts = lax.axis_size("expert")
    _, width = tokens.shape
    wg, wu, wd = w_gate[0], w_up[0], w_down[0]
    first, second = dispatch(expert_ids.T, gate_weights.T, tokens, out_grad, experts, 8)
    first = exchange(first.reshape(experts, 2 * FULL, width))
    first, second = lax.optimization_barrier((first, second))
    second = exchange(second.reshape(experts, 2 * PART, width))
    pick_full, pick_part = picker(expert_ids, gate_weights, experts)
    full, hid_a, dg_a, du_a = main_experts(first, wg, wu, wd, 32)
    part, tok_b, cot_b, hid_b, dg_b, du_b = rest_experts(second, wg, wu, wd)
    full = exchange(full)
    tok = jnp.concatenate([first[:, :FULL].reshape(-1, width), tok_b], axis=0)
    cot = jnp.concatenate([first[:, FULL:].reshape(-1, width), cot_b], axis=0)
    hid = jnp.concatenate([hid_a, hid_b], axis=0)
    d_gate = jnp.concatenate([dg_a, dg_b], axis=0)
    d_up = jnp.concatenate([du_a, du_b], axis=0)
    grad_gate = replica_sum(contract_cols(tok, d_gate).astype(BF16))
    grad_up = replica_sum(contract_cols(tok, d_up).astype(BF16))
    grad_down = replica_sum(contract_cols(hid, cot).astype(BF16))
    full, part, pick_full, pick_part, grad_gate, grad_up = lax.optimization_barrier(
        (full, part, pick_full, pick_part, grad_gate, grad_up)
    )
    full = full.reshape(-1, width)
    part = exchange(part).reshape(-1, width)
    old = gather(pick_full, full, 512)
    mixed, grad_tokens = finish(pick_part, part, old)
    return mixed, grad_tokens, grad_gate[None], grad_up[None], grad_down[None]


def solution(mesh):
    by_row = P(("dp", "expert"), None)
    by_expert = P("expert", None, None)
    return jax.shard_map(
        layer,
        mesh=mesh,
        in_specs=(by_row, by_row, by_row, by_expert, by_expert, by_expert, by_row),
        out_specs=(by_row, by_row, by_expert, by_expert, by_expert),
        check_vma=False,
    )
```

time: 219 us -> 228 us (1.041)
  starting transfers between devices: 16.4 us -> 26.7 us
  waiting for transfers between devices: 57.8 us -> 50.2 us
  matrix products: 11 us -> 14.4 us
    convert_element_type x0 -> x2, other arithmetic: none -> 10.6 us  [replica_sum(): return (part.astype(F32) + other.astype(F32)).astype(BF16)]
    all_to_all x2 -> x3, starting transfers between devices: 15.8 us -> 26.2 us  [exchange(): lax.all_to_all(blocks, 'expert', split_axis=0, concat_axis=0, tiled=True)]
    broadcast_in_dim x3 -> x1, other arithmetic: 15.5 us -> 6.19 us  [layer(): return (mixed, grad_tokens, grad_gate[None], grad_up[None], grad_down[None])]
    all_to_all x2 -> x3, waiting for transfers between devices: 57.8 us -> 50.2 us  [exchange(): lax.all_to_all(blocks, 'expert', split_axis=0, concat_axis=0, tiled=True)]
    dot_general x3, matrix products: 11 us -> 14.4 us  [contract_cols(): lax.dot_general(left, right, (((0,), (0,)), ((), ())), preferred_element_...]
    pallas_call x3 -> x4, Pallas kernels: 23.4 us -> 21.9 us  [the longest x1 12 us: rest_experts(): pl.pallas_call(rest_body, in_specs=[pl.BlockSpec(memory_space=pltpu.VMEM)...]
  transfers between devices with their start and end apart: 5 -> 6, of which waited for: 2 -> 3; matrix products, arithmetic and copies ran while one was open for 14% -> 15% of each run, Pallas kernels for 10% -> 11%
where the time goes in v1:
time: 228 us; the launch traced here: 225 us
  blocking collectives  61.4 us (27%)
  waiting for transfers between devices  50.2 us (22%)
  Pallas kernels  47.3 us (21%)
  starting transfers between devices  26.7 us (12%)
  other arithmetic  16.8 us (7%)
  matrix products  14.4 us (6%)
  local copies, waits for them, and re-layouts  7.57 us (3%)
    all_to_all x1, blocking collectives, exchange(): lax.all_to_all(blocks, 'expert', split_axis=0, concat_axis=0, tiled=True)  61.4 us
    all_to_all x3, waiting for transfers between devices, exchange(): lax.all_to_all(blocks, 'expert', split_axis=0, concat_axis=0, tiled=True)  50.2 us
    all_to_all x3, starting transfers between devices, exchange(): lax.all_to_all(blocks, 'expert', split_axis=0, concat_axis=0, tiled=True)  26.2 us
    pallas_call x1, Pallas kernels, main_experts(): pl.pallas_call(main_body, grid=(sources // group,), in_specs=[pl.BlockSpe...  17.6 us
    dot_general x3, matrix products, contract_cols(): lax.dot_general(left, right, (((0,), (0,)), ((), ())), preferred_element_...  14.4 us
    pallas_call x1, Pallas kernels, rest_experts(): pl.pallas_call(rest_body, in_specs=[pl.BlockSpec(memory_space=pltpu.VMEM)...  12 us
    convert_element_type x2, other arithmetic, replica_sum(): return (part.astype(F32) + other.astype(F32)).astype(BF16)  10.6 us
    pallas_call x1, Pallas kernels, dispatch(): pl.pallas_call(lambda *refs: dispatch_body(per_step, *refs), grid=(expert...  7.8 us
  transfers between devices with their start and end apart: 6, of which 3 were waited for; matrix products, arithmetic and copies ran while one was open for 15% of the time, Pallas kernels for 11%

profile of v1, /device:TPU:4, one launch (start us, length us, event | category | flops | bytes accessed | tf_op | source)
XLA Modules:
  0.0 225.2 jit_solution(5983866088892119557)
XLA Ops:
  0.6 7.8 %dispatch.1 = (bf16[1024,2048]{1,0:T(8,128)(2,1)}, bf16[512,2048]{1,0:T(8,128)(2,1)}) custom-call(s32[4,128]{1,0:T(4,128)} %bitcast.28, f32[4,128]{1,0:T(4,128)} %bitcast.29, bf16[128,2048]{1,0:T(8,128)(2,1)} %refs_2_.1, bf16[128,2048]{1,0:T(8,128)(2,1)} %refs_3_.1), custom_call_target="tpu_custom_call" | custom-call | tf_op jit(solution)/shard_map/dispatch/pallas_call | solution.py:79
  8.4 61.4 %all_to_all.20.tok_ref.cot_ref = bf16[64,16,2048]{2,1,0:T(8,128)(2,1)} all-to-all(bf16[64,16,2048]{2,1,0:T(8,128)(2,1)} %bitcast.24), channel_id=1, replica_groups=mesh['dp'=2,'expert'=64] {'expert'}, dimensions={0} | all-to-all | bytes 8388608 | tf_op jit(solution)/shard_map/all_to_all | solution.py:279
  69.9 7.8 %all-to-all-start.2 = ((bf16[64,8,2048]{2,1,0:T(8,128)(2,1)}), bf16[64,8,2048]{2,1,0:T(8,128)(2,1)S(1)}, u32[]{:S(2)}, u32[]{:S(2)}) async-start(bf16[64,8,2048]{2,1,0:T(8,128)(2,1)} %bitcast.27), calls=%async_computation.2 | async-start | bytes 4194304 | tf_op jit(solution)/shard_map/all_to_all | solution.py:279
  77.7 17.6 %experts_main.1 = (bf16[64,16,2048]{2,1,0:T(8,128)(2,1)}, bf16[512,768]{1,0:T(8,128)(2,1)}, bf16[512,768]{1,0:T(8,128)(2,1)}, bf16[512,768]{1,0:T(8,128)(2,1)}) custom-call(bf16[64,16,2048]{2,1,0:T(8,128)(2,1)} %all_to_all.20.tok_ref.cot_ref, bf16[64,16,2048]{2,1,0:T(8,128)(2,1)} %all_to_all.20.tok_ref.cot_ref, bf16[2048,768]{1,0:T(8,128)(2,1)} %bitcast.18, ...), custom_call_target="tpu_custom_call" | custom-call | tf_op jit(solution)/shard_map/experts_main/pallas_call | solution.py:217
  95.3 4.8 %slice_bitcast_fusion = (bf16[512,2048]{1,0:T(8,128)(2,1)}, bf16[512,2048]{1,0:T(8,128)(2,1)}) fusion(bf16[64,16,2048]{2,1,0:T(8,128)(2,1)} %all_to_all.20.tok_ref.cot_ref), kind=kLoop, calls=%fused_computation.11 | loop fusion | bytes 8388608 | tf_op jit(solution)/shard_map/reshape | solution.py:300
  100.1 3.4 %all-to-all-done.2.mix_ref = bf16[64,8,2048]{2,1,0:T(8,128)(2,1)S(1)} async-done(((bf16[64,8,2048]{2,1,0:T(8,128)(2,1)}), bf16[64,8,2048]{2,1,0:T(8,128)(2,1)S(1)}, u32[]{:S(2)}, u32[]{:S(2)}) %all-to-all-start.2) | async-done | bytes 2097184 | tf_op jit(solution)/shard_map/all_to_all | solution.py:279
  103.5 0.0 copy-start.8
  103.5 0.0 copy-start.12
  103.5 12.0 %experts_rest.1 = (bf16[64,8,2048]{2,1,0:T(8,128)(2,1)}, bf16[256,2048]{1,0:T(8,128)(2,1)S(1)}, bf16[256,2048]{1,0:T(8,128)(2,1)S(1)}, bf16[256,768]{1,0:T(8,128...) custom-call(bf16[64,8,2048]{2,1,0:T(8,128)(2,1)S(1)} %all-to-all-done.2.mix_ref, ...), custom_call_target="tpu_custom_call" | custom-call | tf_op jit(solution)/shard_map/experts_rest/pallas_call | solution.py:269
  115.5 0.0 copy-start.3
  115.5 0.0 copy-start.5
  115.5 0.0 copy-done.8
  115.5 0.0 copy-done.12
  115.5 4.0 %convolution_convert_fusion.1 = bf16[2048,768]{1,0:T(8,128)(2,1)} fusion(bf16[256,2048]{1,0:T(8,128)(2,1)S(1)} %get-tuple-element.39, bf16[512,2048]{1,0:T(8,128)(2,1)S(1)} %copy-done.8, bf16[256,768]{1,0:T(8,128)(2,1)S(1)} %get-tuple-element.43, bf16[512,768]{1,0:T(8,128)(2,1)S(1)} %copy-done.12), kind=kOutput, calls=%fused_computation.4 | convolution fusion | flops 2426142720 | bytes 7471104 | tf_op jit(solution)/shard_map/dot_general | solution.py:25
  119.6 0.0 copy-done.3
  119.6 0.0 copy-done.5
  119.6 0.0 collective-permute-start.1
  119.6 0.0 copy-start.4
  119.6 0.0 copy-start.6
  119.6 8.1 %all-to-all-start.1 = ((bf16[64,16,2048]{2,1,0:T(8,128)(2,1)}), bf16[64,16,2048]{2,1,0:T(8,128)(2,1)}, u32[]{:S(2)}, u32[]{:S(2)}) async-start(bf16[64,16,2048]{2,1,0:T(8,128)(2,1)} %get-tuple-element.34), calls=%async_computation.1 | async-start | bytes 8388608 | tf_op jit(solution)/shard_map/all_to_all | solution.py:279
  127.7 0.0 copy-done.4
  127.7 0.0 copy-done.6
  127.7 0.0 copy-start.7
  127.7 0.0 copy-start.11
  127.7 6.3 %convolution_convert_fusion.2 = bf16[2048,768]{1,0:T(8,128)(2,1)} fusion(bf16[256,2048]{1,0:T(8,128)(2,1)S(1)} %copy-done.4, bf16[512,2048]{1,0:T(8,128)(2,1)} %get-tuple-element.58, bf16[256,768]{1,0:T(8,128)(2,1)S(1)} %copy-done.6, bf16[512,768]{1,0:T(8,128)(2,1)} %get-tuple-element.40), kind=kOutput, calls=%fused_computation.5 | convolution fusion | flops 2426142720 | bytes 7471104 | tf_op jit(solution)/shard_map/dot_general | solution.py:25
  134.0 0.2 collective-permute-start
  134.1 0.0 copy-done.7
  134.2 0.0 copy-done.11
  134.2 0.0 copy-start.9
  134.2 0.0 copy-start.10
  134.2 4.1 %convolution_convert_fusion = bf16[768,2048]{1,0:T(8,128)(2,1)} fusion(bf16[256,2048]{1,0:T(8,128)(2,1)S(1)} %get-tuple-element.56, bf16[512,2048]{1,0:T(8,128)(2,1)S(1)} %copy-done.7, bf16[256,768]{1,0:T(8,128)(2,1)S(1)} %get-tuple-element.55, bf16[512,768]{1,0:T(8,128)(2,1)S(1)} %copy-done.11), kind=kOutput, calls=%fused_computation.3 | convolution fusion | flops 2426142720 | bytes 7471104 | tf_op jit(solution)/shard_map/dot_general | solution.py:25
  138.2 0.3 collective-permute-start.2
  138.6 0.0 copy-done.9
  138.6 0.7 copy.12.refs_0_
  139.3 0.0 copy-done.10
  139.3 0.7 copy.13.refs_1_
  140.0 2.5 %picker.1 = (bf16[384,1024]{1,0:T(8,128)(2,1)}, bf16[384,512]{1,0:T(8,128)(2,1)}) custom-call(s32[128,4]{1,0:T(8,128)} %copy.12.refs_0_, f32[128,4]{1,0:T(8,128)} %copy.13.refs_1_), custom_call_target="tpu_custom_call" | custom-call | tf_op jit(solution)/shard_map/picker/pallas_call | solution.py:132
  142.6 0.0 collective-permute-done.1
  142.6 5.3 %add_convert_fusion.1 = bf16[2048,768]{1,0:T(8,128)(2,1)} fusion(bf16[2048,768]{1,0:T(8,128)(2,1)} %collective-permute-done.1, bf16[2048,768]{1,0:T(8,128)(2,1)} %convolution_convert_fusion.1), kind=kLoop, calls=%fused_computation.1 | loop fusion | flops 6291456 | bytes 9437184 | tf_op jit(solution)/shard_map/convert_element_type | solution.py:284
  147.9 0.0 collective-permute-done
  147.9 5.3 %add_convert_fusion.2 = bf16[2048,768]{1,0:T(8,128)(2,1)} fusion(bf16[2048,768]{1,0:T(8,128)(2,1)} %collective-permute-done, bf16[2048,768]{1,0:T(8,128)(2,1)} %convolution_convert_fusion.2), kind=kLoop, calls=%fused_computation.2 | loop fusion | flops 6291456 | bytes 9437184 | tf_op jit(solution)/shard_map/convert_element_type | solution.py:284
  153.2 31.6 %all-to-all-done.1 = bf16[64,16,2048]{2,1,0:T(8,128)(2,1)} async-done(((bf16[64,16,2048]{2,1,0:T(8,128)(2,1)}), bf16[64,16,2048]{2,1,0:T(8,128)(2,1)}, u32[]{:S(2)}, u32[]{:S(2)}) %all-to-all-start.1) | async-done | bytes 4194336 | tf_op jit(solution)/shard_map/all_to_all | solution.py:279
  184.8 10.3 %all-to-all-start.3 = ((bf16[64,8,2048]{2,1,0:T(8,128)(2,1)}), bf16[64,8,2048]{2,1,0:T(8,128)(2,1)S(1)}, u32[]{:S(2)}, u32[]{:S(2)}) async-start(bf16[64,8,2048]{2,1,0:T(8,128)(2,1)} %get-tuple-element.45), calls=%async_computation.3 | async-start | bytes 4194304 | tf_op jit(solution)/shard_map/all_to_all | solution.py:279
  195.1 5.5 %gather.1 = (f32[128,2048]{1,0:T(8,128)}, f32[128,2048]{1,0:T(8,128)}) custom-call(bf16[384,1024]{1,0:T(8,128)(2,1)} %get-tuple-element.46.pick_ref, bf16[1024,2048]{1,0:T(8,128)(2,1)} %bitcast.9.back_ref), custom_call_target="tpu_custom_call" | custom-call | tf_op jit(solution)/shard_map/gather/pallas_call | solution.py:161
  200.6 0.0 copy-start
  200.6 0.0 copy-start.2
  200.6 0.0 collective-permute-done.2
  200.6 6.2 %fusion = bf16[1,768,2048]{2,1,0:T(8,128)(2,1)} fusion(bf16[768,2048]{1,0:T(8,128)(2,1)} %collective-permute-done.2, bf16[768,2048]{1,0:T(8,128)(2,1)} %convolution_convert_fusion), kind=kLoop, calls=%fused_computation.6 | loop fusion | flops 6291456 | bytes 9437184 | tf_op jit(solution)/shard_map/broadcast_in_dim | solution.py:314
  206.8 15.3 %all-to-all-done.3 = bf16[64,8,2048]{2,1,0:T(8,128)(2,1)S(1)} async-done(((bf16[64,8,2048]{2,1,0:T(8,128)(2,1)}), bf16[64,8,2048]{2,1,0:T(8,128)(2,1)S(1)}, u32[]{:S(2)}, u32[]{:S(2)}) %all-to-all-start.3) | async-done | bytes 2097184 | tf_op jit(solution)/shard_map/all_to_all | solution.py:279
  222.0 0.0 copy-done
  222.0 0.0 copy-done.2
  222.0 0.0 copy-start.1
  222.0 1.2 copy-done.1
  223.3 1.9 finish.1
Async XLA Ops:
  69.9 33.6 %all-to-all-start.2 = ((bf16[64,8,2048]{2,1,0:T(8,128)(2,1)}), bf16[64,8,2048]{2,1,0:T(8,128)(2,1)S(1)}, u32[]{:S(2)}, u32[]{:S(2)}) async-start(bf16[64,8,2048]{2,1,0:T(8,128)(2,1)} %bitcast.27), calls=%async_computation.2 | async-start | bytes 4194304 | tf_op jit(solution)/shard_map/all_to_all | solution.py:279
  103.5 12.0 %copy-start.8 = (bf16[512,2048]{1,0:T(8,128)(2,1)S(1)}, bf16[512,2048]{1,0:T(8,128)(2,1)}, u32[]{:S(2)}) copy-start(bf16[512,2048]{1,0:T(8,128)(2,1)} %get-tuple-element.58) | copy-start | bytes 6291460
  103.5 12.0 %copy-start.12 = (bf16[512,768]{1,0:T(8,128)(2,1)S(1)}, bf16[512,768]{1,0:T(8,128)(2,1)}, u32[]{:S(2)}) copy-start(bf16[512,768]{1,0:T(8,128)(2,1)} %get-tuple-element.42) | copy-start | bytes 2359300
  115.5 4.1 %copy-start.3 = (bf16[256,2048]{1,0:T(8,128)(2,1)}, bf16[256,2048]{1,0:T(8,128)(2,1)S(1)}, u32[]{:S(2)}) copy-start(bf16[256,2048]{1,0:T(8,128)(2,1)S(1)} %get-tuple-element.39) | copy-start | bytes 3145732
  115.5 4.1 %copy-start.5 = (bf16[256,768]{1,0:T(8,128)(2,1)}, bf16[256,768]{1,0:T(8,128)(2,1)S(1)}, u32[]{:S(2)}) copy-start(bf16[256,768]{1,0:T(8,128)(2,1)S(1)} %get-tuple-element.41) | copy-start | bytes 1179652
  119.6 23.0 %collective-permute-start.1 = (bf16[2048,768]{1,0:T(8,128)(2,1)}, bf16[2048,768]{1,0:T(8,128)(2,1)}, u32[]{:S(2)}, u32[]{:S(2)}) collective-permute-start(bf16[2048,768]{1,0:T(8,128)(2,1)} %convolution_convert_fusion.1), channel_id=1, source_target_pairs={{0,64},{64,0},{1,65},{65,1},{2,66},{66,2},{3,67},{67,3},{4,68},{68... | collective-permute-start | bytes 9437192 | tf_op jit(solution)/shard_map/ppermute | solution.py:283
  119.6 8.1 %copy-start.4 = (bf16[256,2048]{1,0:T(8,128)(2,1)S(1)}, bf16[256,2048]{1,0:T(8,128)(2,1)}, u32[]{:S(2)}) copy-start(bf16[256,2048]{1,0:T(8,128)(2,1)} %copy-done.3) | copy-start | bytes 3145732
  119.6 8.1 %copy-start.6 = (bf16[256,768]{1,0:T(8,128)(2,1)S(1)}, bf16[256,768]{1,0:T(8,128)(2,1)}, u32[]{:S(2)}) copy-start(bf16[256,768]{1,0:T(8,128)(2,1)} %copy-done.5) | copy-start | bytes 1179652
  119.6 65.2 %all-to-all-start.1 = ((bf16[64,16,2048]{2,1,0:T(8,128)(2,1)}), bf16[64,16,2048]{2,1,0:T(8,128)(2,1)}, u32[]{:S(2)}, u32[]{:S(2)}) async-start(bf16[64,16,2048]{2,1,0:T(8,128)(2,1)} %get-tuple-element.34), calls=%async_computation.1 | async-start | bytes 8388608 | tf_op jit(solution)/shard_map/all_to_all | solution.py:279
  127.7 6.5 %copy-start.7 = (bf16[512,2048]{1,0:T(8,128)(2,1)S(1)}, bf16[512,2048]{1,0:T(8,128)(2,1)}, u32[]{:S(2)}) copy-start(bf16[512,2048]{1,0:T(8,128)(2,1)} %get-tuple-element.57) | copy-start | bytes 6291460
  127.7 6.5 %copy-start.11 = (bf16[512,768]{1,0:T(8,128)(2,1)S(1)}, bf16[512,768]{1,0:T(8,128)(2,1)}, u32[]{:S(2)}) copy-start(bf16[512,768]{1,0:T(8,128)(2,1)} %get-tuple-element.54) | copy-start | bytes 2359300
  134.0 13.9 %collective-permute-start = (bf16[2048,768]{1,0:T(8,128)(2,1)}, bf16[2048,768]{1,0:T(8,128)(2,1)}, u32[]{:S(2)}, u32[]{:S(2)}) collective-permute-start(bf16[2048,768]{1,0:T(8,128)(2,1)} %convolution_convert_fusion.2), channel_id=1, source_target_pairs={{0,64},{64,0},{1,65},{65,1},{2,66},{66,2},{3,67},{67,3},{4,68},{68... | collective-permute-start | bytes 9437192 | tf_op jit(solution)/shard_map/ppermute | solution.py:283
  134.2 4.4 %copy-start.9 = (s32[128,4]{0,1:T(4,128)S(1)}, s32[128,4]{0,1:T(4,128)}, u32[]{:S(2)}) copy-start(s32[128,4]{0,1:T(4,128)} %param.8) | copy-start | bytes 6148
  134.2 5.1 %copy-start.10 = (f32[128,4]{0,1:T(4,128)S(1)}, f32[128,4]{0,1:T(4,128)}, u32[]{:S(2)}) copy-start(f32[128,4]{0,1:T(4,128)} %param.9) | copy-start | bytes 6148
  138.2 62.4 %collective-permute-start.2 = (bf16[768,2048]{1,0:T(8,128)(2,1)}, bf16[768,2048]{1,0:T(8,128)(2,1)}, u32[]{:S(2)}, u32[]{:S(2)}) collective-permute-start(bf16[768,2048]{1,0:T(8,128)(2,1)} %convolution_convert_fusion), channel_id=1, source_target_pairs={{0,64},{64,0},{1,65},{65,1},{2,66},{66,2},{3,67},{67,3},{4,68},{68... | collective-permute-start | bytes 9437192 | tf_op jit(solution)/shard_map/ppermute | solution.py:283
  184.8 37.3 %all-to-all-start.3 = ((bf16[64,8,2048]{2,1,0:T(8,128)(2,1)}), bf16[64,8,2048]{2,1,0:T(8,128)(2,1)S(1)}, u32[]{:S(2)}, u32[]{:S(2)}) async-start(bf16[64,8,2048]{2,1,0:T(8,128)(2,1)} %get-tuple-element.45), calls=%async_computation.3 | async-start | bytes 4194304 | tf_op jit(solution)/shard_map/all_to_all | solution.py:279
  200.6 21.5 %copy-start = (f32[128,2048]{1,0:T(8,128)S(1)}, f32[128,2048]{1,0:T(8,128)}, u32[]{:S(2)}) copy-start(f32[128,2048]{1,0:T(8,128)} %get-tuple-element.48.mixed_old_ref) | copy-start | bytes 3145732
  200.6 21.5 %copy-start.2 = (bf16[384,512]{1,0:T(8,128)(2,1)S(1)}, bf16[384,512]{1,0:T(8,128)(2,1)}, u32[]{:S(2)}) copy-start(bf16[384,512]{1,0:T(8,128)(2,1)} %get-tuple-element.44.pick_ref) | copy-start | bytes 1179652
  222.0 1.2 copy-start.1

commit v2 on v1

--- a/solution.py
+++ b/solution.py
@@ -29,21 +29,22 @@
     return lax.broadcasted_iota(jnp.int32, shape, dim)
 
 
-def dispatch_body(experts, ids_ref, gates_ref, tokens_ref, grad_ref, first_ref, second_ref, both_ref, sems):
-    rows = tokens_ref.shape[0]
-
-    @pl.when(pl.program_id(0) == 0)
-    def _():
-        copies = [
-            pltpu.make_async_copy(tokens_ref, both_ref.at[pl.ds(0, rows)], sems.at[0]),
-            pltpu.make_async_copy(grad_ref, both_ref.at[pl.ds(rows, rows)], sems.at[1]),
-        ]
-        for copy in copies:
-            copy.start()
-        for copy in copies:
-            copy.wait()
-
-    expert = iota((experts, rows), 0) + pl.program_id(0) * experts
+def dispatch_body(experts, parts, ids_hbm, gates_hbm, tokens_hbm, grad_hbm, first_hbm, second_hbm, *scratch):
+    ids_ref, gates_ref, both_ref, first_ref, second_ref, in_sems, out_sems = scratch
+    rows = tokens_hbm.shape[0]
+    early = [
+        pltpu.make_async_copy(ids_hbm, ids_ref, in_sems.at[0]),
+        pltpu.make_async_copy(gates_hbm, gates_ref, in_sems.at[1]),
+    ]
+    late = [
+        pltpu.make_async_copy(tokens_hbm, both_ref.at[pl.ds(0, rows)], in_sems.at[2]),
+        pltpu.make_async_copy(grad_hbm, both_ref.at[pl.ds(rows, rows)], in_sems.at[3]),
+    ]
+    for copy in early + late:
+        copy.start()
+    for copy in early:
+        copy.wait()
+    expert = iota((experts, rows), 0)
     member = jnp.zeros((experts, rows), F32)
     gate = jnp.zeros((experts, rows), F32)
     for k in range(ids_ref.shape[0]):
@@ -53,47 +54,52 @@
     earlier = jnp.where(iota((rows, rows), 0) < iota((rows, rows), 1), 1.0, 0.0).astype(BF16)
     rank = jnp.where(member > 0.5, dot(member.astype(BF16), earlier), NO_SLOT)
 
-    def fill(out_ref, depth, base):
-        shape = (experts, 2 * depth, rows)
-        flat = (experts * 2 * depth, rows)
+    def picks(depth, base, low, high):
+        shape = (high - low, 2 * depth, rows)
+        flat = ((high - low) * 2 * depth, rows)
         row = iota(shape, 1)
         slot = (jnp.where(row < depth, row, row - depth) + base).astype(F32)
         is_token = row < depth
-        hit = rank[:, None, :] == slot
+        hit = rank[low:high, None, :] == slot
         one = jnp.where(hit, 1.0, 0.0)
         of_token = jnp.where(is_token, one, 0.0).reshape(flat)
         of_grad = jnp.where(is_token, 0.0, one).reshape(flat)
-        scale = jnp.where(hit, jnp.broadcast_to(gate[:, None, :], shape), 0.0)
+        scale = jnp.where(hit, jnp.broadcast_to(gate[low:high, None, :], shape), 0.0)
         scale = jnp.sum(jnp.where(is_token, one, scale).reshape(flat), axis=1, keepdims=True)
-        pick = jnp.concatenate([of_token, of_grad], axis=1).astype(BF16)
-        out_ref[...] = (dot(pick, both_ref[...]) * scale).astype(BF16)
-
-    fill(first_ref, FULL, 0)
-    fill(second_ref, PART, FULL)
-
-
-def dispatch(ids_t, gates_t, tokens, out_grad, experts, per_step):
+        return jnp.concatenate([of_token, of_grad], axis=1).astype(BF16), scale
+
+    per = experts // parts
+    stores = []
+    for p in range(parts):
+        for depth, base, buf, out in ((FULL, 0, first_ref, first_hbm), (PART, FULL, second_ref, second_hbm)):
+            pick, scale = picks(depth, base, p * per, (p + 1) * per)
+            if not stores:
+                for copy in late:
+                    copy.wait()
+            span = pl.ds(p * per * 2 * depth, per * 2 * depth)
+            buf[span] = (dot(pick, both_ref[...]) * scale).astype(BF16)
+            stores.append(pltpu.make_async_copy(buf.at[span], out.at[span], out_sems.at[len(stores)]))
+            stores[-1].start()
+    for store in stores:
+        store.wait()
+
+
+def dispatch(ids_t, gates_t, tokens, out_grad, experts, parts):
     rows, width = tokens.shape
-    top = ids_t.shape[0]
-    whole = lambda shape: pl.BlockSpec(shape, lambda i: (0, 0))
-    return pl.pallas_call(
-        lambda *refs: dispatch_body(per_step, *refs),
-        grid=(experts // per_step,),
-        in_specs=[
-            whole((top, rows)),
-            whole((top, rows)),
-            pl.BlockSpec(memory_space=pl.ANY),
-            pl.BlockSpec(memory_space=pl.ANY),
-        ],
-        out_specs=[
-            pl.BlockSpec((per_step * 2 * FULL, width), lambda i: (i, 0)),
-            pl.BlockSpec((per_step * 2 * PART, width), lambda i: (i, 0)),
-        ],
-        out_shape=[
-            jax.ShapeDtypeStruct((experts * 2 * FULL, width), BF16),
-            jax.ShapeDtypeStruct((experts * 2 * PART, width), BF16),
-        ],
-        scratch_shapes=[pltpu.VMEM((2 * rows, width), BF16), pltpu.SemaphoreType.DMA((2,))],
+    shapes = [(experts * 2 * FULL, width), (experts * 2 * PART, width)]
+    anywhere = pl.BlockSpec(memory_space=pl.ANY)
+    return pl.pallas_call(
+        lambda *refs: dispatch_body(experts, parts, *refs),
+        in_specs=[anywhere] * 4,
+        out_specs=[anywhere] * 2,
+        out_shape=[jax.ShapeDtypeStruct(shape, BF16) for shape in shapes],
+        scratch_shapes=[
+            pltpu.VMEM(ids_t.shape, ids_t.dtype),
+            pltpu.VMEM(gates_t.shape, gates_t.dtype),
+            pltpu.VMEM((2 * rows, width), BF16),
+        ]
+        + [pltpu.VMEM(shape, BF16) for shape in shapes]
+        + [pltpu.SemaphoreType.DMA((4,)), pltpu.SemaphoreType.DMA((2 * parts,))],
         name="dispatch",
     )(ids_t, gates_t, tokens, out_grad)
 
@@ -146,37 +152,60 @@
     grad_ref[...] = total[2 * rows : 3 * rows]
 
 
-def finish_body(pick_ref, back_ref, mixed_old_ref, grad_old_ref, mixed_ref, grad_ref):
-    rows = mixed_ref.shape[0]
-    total = dot(pick_ref[...], back_ref[...])
-    mixed_ref[...] = (mixed_old_ref[...] + total[0:rows] + total[rows : 2 * rows]).astype(BF16)
-    grad_ref[...] = (grad_old_ref[...] + total[2 * rows : 3 * rows]).astype(BF16)
-
-
-def gather(pick, back, cols):
-    rows = pick.shape[0] // 3
-    total, width = back.shape
-    out = jax.ShapeDtypeStruct((rows, width), F32)
-    by_cols = lambda count: pl.BlockSpec((count, cols), lambda i: (0, i))
+def finish_body(parts, pick_ref, back_ref, mixed_old_ref, grad_old_hbm, mixed_hbm, grad_hbm, *scratch):
+    grad_old_ref, mixed_ref, grad_ref, sem, sems = scratch
+    load = pltpu.make_async_copy(grad_old_hbm, grad_old_ref, sem)
+    load.start()
+    rows, width = mixed_ref.shape
+    stores = []
+    cols = width // parts
+    for p in range(parts):
+        low, high = p * cols, (p + 1) * cols
+        total = dot(pick_ref[...], back_ref[:, low:high])
+        mixed = mixed_old_ref[:, low:high] + total[0:rows] + total[rows : 2 * rows]
+        mixed_ref[:, low:high] = mixed.astype(BF16)
+        if not stores:
+            load.wait()
+        grad_ref[:, low:high] = (grad_old_ref[:, low:high] + total[2 * rows : 3 * rows]).astype(BF16)
+        for ref, out in ((mixed_ref, mixed_hbm), (grad_ref, grad_hbm)):
+            span = pl.ds(low, cols)
+            stores.append(pltpu.make_async_copy(ref.at[:, span], out.at[:, span], sems.at[len(stores)]))
+            stores[-1].start()
+    for store in stores:
+        store.wait()
+
+
+def gather(pick, back):
+    shape = (pick.shape[0] // 3, back.shape[1])
+    vmem = pl.BlockSpec(memory_space=pltpu.VMEM)
     return pl.pallas_call(
         gather_body,
-        grid=(width // cols,),
-        in_specs=[pl.BlockSpec(pick.shape, lambda i: (0, 0)), by_cols(total)],
-        out_specs=[by_cols(rows)] * 2,
-        out_shape=[out, out],
+        in_specs=[vmem] * 2,
+        out_specs=[vmem] * 2,
+        out_shape=[pltpu.VMEM(shape, F32), jax.ShapeDtypeStruct(shape, F32)],
+        compiler_params=pltpu.CompilerParams(vmem_limit_bytes=40 << 20),
         name="gather",
     )(pick, back)
 
 
-def finish(pick, back, old):
-    out = jax.ShapeDtypeStruct(old[0].shape, BF16)
-    return pl.pallas_call(
-        finish_body,
-        in_specs=[pl.BlockSpec(memory_space=pltpu.VMEM)] * 4,
-        out_shape=[out, out],
+def finish(pick, back, old, parts):
+    shape = old[0].shape
+    anywhere = pl.BlockSpec(memory_space=pl.ANY)
+    return pl.pallas_call(
+        lambda *refs: finish_body(parts, *refs),
+        in_specs=[pl.BlockSpec(memory_space=pltpu.VMEM)] * 3 + [pl.BlockSpec(memory_space=pltpu.HBM)],
+        out_specs=[anywhere] * 2,
+        out_shape=[jax.ShapeDtypeStruct(shape, BF16)] * 2,
+        scratch_shapes=[pltpu.VMEM(shape, F32)]
+        + [pltpu.VMEM(shape, BF16)] * 2
+        + [pltpu.SemaphoreType.DMA(()), pltpu.SemaphoreType.DMA((2 * parts,))],
         compiler_params=pltpu.CompilerParams(vmem_limit_bytes=24 << 20),
         name="finish",
-    )(*map(in_vmem, (pick, back, *old)))
+    )(in_vmem(pick), in_vmem(back), in_vmem(old[0]), in_hbm(old[1]))
+
+
+def in_hbm(array):
+    return pltpu.with_memory_space_constraint(array, pltpu.HBM)
 
 
 def in_vmem(array):
@@ -288,7 +317,7 @@
     experts = lax.axis_size("expert")
     _, width = tokens.shape
     wg, wu, wd = w_gate[0], w_up[0], w_down[0]
-    first, second = dispatch(expert_ids.T, gate_weights.T, tokens, out_grad, experts, 8)
+    first, second = dispatch(expert_ids.T, gate_weights.T, tokens, out_grad, experts, 4)
     first = exchange(first.reshape(experts, 2 * FULL, width))
     first, second = lax.optimization_barrier((first, second))
     second = exchange(second.reshape(experts, 2 * PART, width))
@@ -309,8 +338,9 @@
     )
     full = full.reshape(-1, width)
     part = exchange(part).reshape(-1, width)
-    old = gather(pick_full, full, 512)
-    mixed, grad_tokens = finish(pick_part, part, old)
+    full, grad_down = lax.optimization_barrier((full, grad_down))
+    old = gather(pick_full, full)
+    mixed, grad_tokens = finish(pick_part, part, old, 2)
     return mixed, grad_tokens, grad_gate[None], grad_up[None], grad_down[None]
 
 

time: 228 us -> 225 us (0.987)
  Pallas kernels: 47.3 us -> 43.2 us
    broadcast_in_dim x1 -> x0, other arithmetic: 6.19 us -> none  [layer(): return (mixed, grad_tokens, grad_gate[None], grad_up[None], grad_down[None])]
    convert_element_type x2 -> x3, other arithmetic: 10.6 us -> 16.7 us  [replica_sum(): return (part.astype(F32) + other.astype(F32)).astype(BF16)]
    pallas_call x3, Pallas kernels: 15.2 us -> 11.1 us  [the longest x1 4.43 us: dispatch(): pl.pallas_call(lambda *refs: dispatch_body(experts, parts, *refs), in_spe...]
where the time goes in v2:
time: 225 us; the launch traced here: 222 us
  blocking collectives  61.5 us (27%)
  waiting for transfers between devices  50.6 us (22%)
  Pallas kernels  43.2 us (19%)
  starting transfers between devices  26.6 us (12%)
  other arithmetic  16.7 us (7%)
  matrix products  14.4 us (6%)
  local copies, waits for them, and re-layouts  7.46 us (3%)
    all_to_all x1, blocking collectives, exchange(): lax.all_to_all(blocks, 'expert', split_axis=0, concat_axis=0, tiled=True)  61.5 us
    all_to_all x3, waiting for transfers between devices, exchange(): lax.all_to_all(blocks, 'expert', split_axis=0, concat_axis=0, tiled=True)  50.6 us
    all_to_all x3, starting transfers between devices, exchange(): lax.all_to_all(blocks, 'expert', split_axis=0, concat_axis=0, tiled=True)  26.1 us
    pallas_call x1, Pallas kernels, main_experts(): pl.pallas_call(main_body, grid=(sources // group,), in_specs=[pl.BlockSpe...  17.6 us
    convert_element_type x3, other arithmetic, replica_sum(): return (part.astype(F32) + other.astype(F32)).astype(BF16)  16.7 us
    dot_general x3, matrix products, contract_cols(): lax.dot_general(left, right, (((0,), (0,)), ((), ())), preferred_element_...  14.4 us
    pallas_call x1, Pallas kernels, rest_experts(): pl.pallas_call(rest_body, in_specs=[pl.BlockSpec(memory_space=pltpu.VMEM)...  12 us
    reshape x1, local copies, waits for them, and re-layouts, layer(): cot = jnp.concatenate([first[:, FULL:].reshape(-1, width), cot_b], axis=0)  4.92 us
  transfers between devices with their start and end apart: 6, of which 3 were waited for; matrix products, arithmetic and copies ran while one was open for 15% of the time, Pallas kernels for 11%

profile of v2, /device:TPU:4, one launch (start us, length us, event | category | flops | bytes accessed | tf_op | source)
XLA Modules:
  0.0 221.5 jit_solution(3970546238074339467)
XLA Ops:
  0.6 4.4 %dispatch.1 = (bf16[1024,2048]{1,0:T(8,128)(2,1)}, bf16[512,2048]{1,0:T(8,128)(2,1)}) custom-call(s32[4,128]{1,0:T(4,128)} %bitcast.28, f32[4,128]{1,0:T(4,128)} %bitcast.29, bf16[128,2048]{1,0:T(8,128)(2,1)} %refs_2_.1, bf16[128,2048]{1,0:T(8,128)(2,1)} %refs_3_.1), custom_call_target="tpu_custom_call" | custom-call | tf_op jit(solution)/shard_map/dispatch/pallas_call | solution.py:91
  5.1 61.5 %all_to_all.20.tok_ref.cot_ref = bf16[64,16,2048]{2,1,0:T(8,128)(2,1)} all-to-all(bf16[64,16,2048]{2,1,0:T(8,128)(2,1)} %bitcast.23), channel_id=1, replica_groups=mesh['dp'=2,'expert'=64] {'expert'}, dimensions={0} | all-to-all | bytes 8388608 | tf_op jit(solution)/shard_map/all_to_all | solution.py:308
  66.6 7.7 %all-to-all-start.2 = ((bf16[64,8,2048]{2,1,0:T(8,128)(2,1)}), bf16[64,8,2048]{2,1,0:T(8,128)(2,1)S(1)}, u32[]{:S(2)}, u32[]{:S(2)}) async-start(bf16[64,8,2048]{2,1,0:T(8,128)(2,1)} %bitcast.27), calls=%async_computation.2 | async-start | bytes 4194304 | tf_op jit(solution)/shard_map/all_to_all | solution.py:308
  74.4 17.6 %experts_main.1 = (bf16[64,16,2048]{2,1,0:T(8,128)(2,1)}, bf16[512,768]{1,0:T(8,128)(2,1)}, bf16[512,768]{1,0:T(8,128)(2,1)}, bf16[512,768]{1,0:T(8,128)(2,1)}) custom-call(bf16[64,16,2048]{2,1,0:T(8,128)(2,1)} %all_to_all.20.tok_ref.cot_ref, bf16[64,16,2048]{2,1,0:T(8,128)(2,1)} %all_to_all.20.tok_ref.cot_ref, bf16[2048,768]{1,0:T(8,128)(2,1)} %bitcast.17, ...), custom_call_target="tpu_custom_call" | custom-call | tf_op jit(solution)/shard_map/experts_main/pallas_call | solution.py:246
  91.9 4.9 %slice_bitcast_fusion = (bf16[512,2048]{1,0:T(8,128)(2,1)}, bf16[512,2048]{1,0:T(8,128)(2,1)}) fusion(bf16[64,16,2048]{2,1,0:T(8,128)(2,1)} %all_to_all.20.tok_ref.cot_ref), kind=kLoop, calls=%fused_computation.10 | loop fusion | bytes 8388608 | tf_op jit(solution)/shard_map/reshape | solution.py:329
  96.9 3.3 %all-to-all-done.2.mix_ref = bf16[64,8,2048]{2,1,0:T(8,128)(2,1)S(1)} async-done(((bf16[64,8,2048]{2,1,0:T(8,128)(2,1)}), bf16[64,8,2048]{2,1,0:T(8,128)(2,1)S(1)}, u32[]{:S(2)}, u32[]{:S(2)}) %all-to-all-start.2) | async-done | bytes 2097184 | tf_op jit(solution)/shard_map/all_to_all | solution.py:308
  100.1 0.0 copy-start.8
  100.1 0.0 copy-start.12
  100.1 12.0 %experts_rest.1 = (bf16[64,8,2048]{2,1,0:T(8,128)(2,1)}, bf16[256,2048]{1,0:T(8,128)(2,1)S(1)}, bf16[256,2048]{1,0:T(8,128)(2,1)S(1)}, bf16[256,768]{1,0:T(8,128...) custom-call(bf16[64,8,2048]{2,1,0:T(8,128)(2,1)S(1)} %all-to-all-done.2.mix_ref, ...), custom_call_target="tpu_custom_call" | custom-call | tf_op jit(solution)/shard_map/experts_rest/pallas_call | solution.py:298
  112.2 0.0 copy-start.3
  112.2 0.0 copy-start.5
  112.2 0.0 copy-done.8
  112.2 0.0 copy-done.12
  112.2 4.0 %convolution_convert_fusion.1 = bf16[2048,768]{1,0:T(8,128)(2,1)} fusion(bf16[256,2048]{1,0:T(8,128)(2,1)S(1)} %get-tuple-element.41, bf16[512,2048]{1,0:T(8,128)(2,1)S(1)} %copy-done.8, bf16[256,768]{1,0:T(8,128)(2,1)S(1)} %get-tuple-element.45, bf16[512,768]{1,0:T(8,128)(2,1)S(1)} %copy-done.12), kind=kOutput, calls=%fused_computation.4 | convolution fusion | flops 2426142720 | bytes 7471104 | tf_op jit(solution)/shard_map/dot_general | solution.py:25
  116.2 0.0 copy-done.3
  116.2 0.0 copy-done.5
  116.2 0.0 collective-permute-start.1
  116.2 0.0 copy-start.4
  116.3 0.0 copy-start.6
  116.3 8.1 %all-to-all-start.1 = ((bf16[64,16,2048]{2,1,0:T(8,128)(2,1)}), bf16[64,16,2048]{2,1,0:T(8,128)(2,1)}, u32[]{:S(2)}, u32[]{:S(2)}) async-start(bf16[64,16,2048]{2,1,0:T(8,128)(2,1)} %get-tuple-element.36), calls=%async_computation.1 | async-start | bytes 8388608 | tf_op jit(solution)/shard_map/all_to_all | solution.py:308
  124.3 0.0 copy-done.4
  124.3 0.0 copy-done.6
  124.3 0.0 copy-start.7
  124.4 0.0 copy-start.11
  124.4 6.3 %convolution_convert_fusion.2 = bf16[2048,768]{1,0:T(8,128)(2,1)} fusion(bf16[256,2048]{1,0:T(8,128)(2,1)S(1)} %copy-done.4, bf16[512,2048]{1,0:T(8,128)(2,1)} %get-tuple-element.62, bf16[256,768]{1,0:T(8,128)(2,1)S(1)} %copy-done.6, bf16[512,768]{1,0:T(8,128)(2,1)} %get-tuple-element.42), kind=kOutput, calls=%fused_computation.5 | convolution fusion | flops 2426142720 | bytes 7471104 | tf_op jit(solution)/shard_map/dot_general | solution.py:25
  130.6 0.2 collective-permute-start
  130.8 0.0 copy-done.7
  130.8 0.0 copy-done.11
  130.8 0.0 copy-start.9
  130.8 0.0 copy-start.10
  130.8 4.1 %convolution_convert_fusion = bf16[768,2048]{1,0:T(8,128)(2,1)} fusion(bf16[256,2048]{1,0:T(8,128)(2,1)S(1)} %get-tuple-element.52, bf16[512,2048]{1,0:T(8,128)(2,1)S(1)} %copy-done.7, bf16[256,768]{1,0:T(8,128)(2,1)S(1)} %get-tuple-element.51, bf16[512,768]{1,0:T(8,128)(2,1)S(1)} %copy-done.11), kind=kOutput, calls=%fused_computation.3 | convolution fusion | flops 2426142720 | bytes 7471104 | tf_op jit(solution)/shard_map/dot_general | solution.py:25
  134.9 0.3 collective-permute-start.2
  135.2 0.0 copy-done.9
  135.2 0.7 copy.12.refs_0_
  136.0 0.0 copy-done.10
  136.0 0.7 copy.13.refs_1_
  136.7 2.5 %picker.1 = (bf16[384,1024]{1,0:T(8,128)(2,1)}, bf16[384,512]{1,0:T(8,128)(2,1)}) custom-call(s32[128,4]{1,0:T(8,128)} %copy.12.refs_0_, f32[128,4]{1,0:T(8,128)} %copy.13.refs_1_), custom_call_target="tpu_custom_call" | custom-call | tf_op jit(solution)/shard_map/picker/pallas_call | solution.py:138
  139.2 0.0 collective-permute-done.1
  139.2 5.3 %add_convert_fusion.1 = bf16[2048,768]{1,0:T(8,128)(2,1)} fusion(bf16[2048,768]{1,0:T(8,128)(2,1)} %collective-permute-done.1, bf16[2048,768]{1,0:T(8,128)(2,1)} %convolution_convert_fusion.1), kind=kLoop, calls=%fused_computation.1 | loop fusion | flops 6291456 | bytes 9437184 | tf_op jit(solution)/shard_map/convert_element_type | solution.py:313
  144.5 0.0 collective-permute-done
  144.6 5.3 %add_convert_fusion.2 = bf16[2048,768]{1,0:T(8,128)(2,1)} fusion(bf16[2048,768]{1,0:T(8,128)(2,1)} %collective-permute-done, bf16[2048,768]{1,0:T(8,128)(2,1)} %convolution_convert_fusion.2), kind=kLoop, calls=%fused_computation.2 | loop fusion | flops 6291456 | bytes 9437184 | tf_op jit(solution)/shard_map/convert_element_type | solution.py:313
  149.8 31.6 %all-to-all-done.1 = bf16[64,16,2048]{2,1,0:T(8,128)(2,1)} async-done(((bf16[64,16,2048]{2,1,0:T(8,128)(2,1)}), bf16[64,16,2048]{2,1,0:T(8,128)(2,1)}, u32[]{:S(2)}, u32[]{:S(2)}) %all-to-all-start.1) | async-done | bytes 4194336 | tf_op jit(solution)/shard_map/all_to_all | solution.py:308
  181.5 10.3 %all-to-all-start.3 = ((bf16[64,8,2048]{2,1,0:T(8,128)(2,1)}), bf16[64,8,2048]{2,1,0:T(8,128)(2,1)S(1)}, u32[]{:S(2)}, u32[]{:S(2)}) async-start(bf16[64,8,2048]{2,1,0:T(8,128)(2,1)} %get-tuple-element.47), calls=%async_computation.3 | async-start | bytes 4194304 | tf_op jit(solution)/shard_map/all_to_all | solution.py:308
  191.8 0.0 copy-start.1
  191.8 0.0 collective-permute-done.2
  191.8 6.2 %add_convert_fusion = bf16[768,2048]{1,0:T(8,128)(2,1)} fusion(bf16[768,2048]{1,0:T(8,128)(2,1)} %collective-permute-done.2, bf16[768,2048]{1,0:T(8,128)(2,1)} %convolution_convert_fusion), kind=kLoop, calls=%fused_computation | loop fusion | flops 6291456 | bytes 9437184 | tf_op jit(solution)/shard_map/convert_element_type | solution.py:313
  198.0 0.0 copy-start.2
  198.0 0.0 copy-done.1
  198.0 4.0 %gather.1 = (f32[128,2048]{1,0:T(8,128)S(1)}, f32[128,2048]{1,0:T(8,128)S(1)}) custom-call(bf16[384,1024]{1,0:T(8,128)(2,1)S(1)} %copy-done.1, bf16[1024,2048]{1,0:T(8,128)(2,1)} %bitcast.9.back_ref), custom_call_target="tpu_custom_call" | custom-call | tf_op jit(solution)/shard_map/gather/pallas_call | solution.py:181
  202.0 0.0 copy-start
  202.0 1.0 copy-done
  203.0 15.7 %all-to-all-done.3 = bf16[64,8,2048]{2,1,0:T(8,128)(2,1)S(1)} async-done(((bf16[64,8,2048]{2,1,0:T(8,128)(2,1)}), bf16[64,8,2048]{2,1,0:T(8,128)(2,1)S(1)}, u32[]{:S(2)}, u32[]{:S(2)}) %all-to-all-start.3) | async-done | bytes 2097184 | tf_op jit(solution)/shard_map/all_to_all | solution.py:308
  218.7 0.0 copy-done.2
  218.7 2.6 %finish.1 = (bf16[128,2048]{1,0:T(8,128)(2,1)}, bf16[128,2048]{1,0:T(8,128)(2,1)}) custom-call(bf16[384,512]{1,0:T(8,128)(2,1)S(1)} %copy-done.2, bf16[512,2048]{1,0:T(8,128)(2,1)S(1)} %bitcast.16, f32[128,2048]{1,0:T(8,128)S(1)} %get-tuple-element.54.refs_2_, f32[128,2048]{1,0:T(8,128)} %copy-done), custom_call_target="tpu_custom_call" | custom-call | tf_op jit(solution)/shard_map/finish/pallas_call | solution.py:194
Async XLA Ops:
  66.6 33.5 %all-to-all-start.2 = ((bf16[64,8,2048]{2,1,0:T(8,128)(2,1)}), bf16[64,8,2048]{2,1,0:T(8,128)(2,1)S(1)}, u32[]{:S(2)}, u32[]{:S(2)}) async-start(bf16[64,8,2048]{2,1,0:T(8,128)(2,1)} %bitcast.27), calls=%async_computation.2 | async-start | bytes 4194304 | tf_op jit(solution)/shard_map/all_to_all | solution.py:308
  100.1 12.0 %copy-start.8 = (bf16[512,2048]{1,0:T(8,128)(2,1)S(1)}, bf16[512,2048]{1,0:T(8,128)(2,1)}, u32[]{:S(2)}) copy-start(bf16[512,2048]{1,0:T(8,128)(2,1)} %get-tuple-element.62) | copy-start | bytes 6291460
  100.1 12.0 %copy-start.12 = (bf16[512,768]{1,0:T(8,128)(2,1)S(1)}, bf16[512,768]{1,0:T(8,128)(2,1)}, u32[]{:S(2)}) copy-start(bf16[512,768]{1,0:T(8,128)(2,1)} %get-tuple-element.44) | copy-start | bytes 2359300
  112.2 4.1 %copy-start.3 = (bf16[256,2048]{1,0:T(8,128)(2,1)}, bf16[256,2048]{1,0:T(8,128)(2,1)S(1)}, u32[]{:S(2)}) copy-start(bf16[256,2048]{1,0:T(8,128)(2,1)S(1)} %get-tuple-element.41) | copy-start | bytes 3145732
  112.2 4.1 %copy-start.5 = (bf16[256,768]{1,0:T(8,128)(2,1)}, bf16[256,768]{1,0:T(8,128)(2,1)S(1)}, u32[]{:S(2)}) copy-start(bf16[256,768]{1,0:T(8,128)(2,1)S(1)} %get-tuple-element.43) | copy-start | bytes 1179652
  116.2 23.0 %collective-permute-start.1 = (bf16[2048,768]{1,0:T(8,128)(2,1)}, bf16[2048,768]{1,0:T(8,128)(2,1)}, u32[]{:S(2)}, u32[]{:S(2)}) collective-permute-start(bf16[2048,768]{1,0:T(8,128)(2,1)} %convolution_convert_fusion.1), channel_id=1, source_target_pairs={{0,64},{64,0},{1,65},{65,1},{2,66},{66,2},{3,67},{67,3},{4,68},{68... | collective-permute-start | bytes 9437192 | tf_op jit(solution)/shard_map/ppermute | solution.py:312
  116.2 8.1 %copy-start.4 = (bf16[256,2048]{1,0:T(8,128)(2,1)S(1)}, bf16[256,2048]{1,0:T(8,128)(2,1)}, u32[]{:S(2)}) copy-start(bf16[256,2048]{1,0:T(8,128)(2,1)} %copy-done.3) | copy-start | bytes 3145732
  116.3 8.1 %copy-start.6 = (bf16[256,768]{1,0:T(8,128)(2,1)S(1)}, bf16[256,768]{1,0:T(8,128)(2,1)}, u32[]{:S(2)}) copy-start(bf16[256,768]{1,0:T(8,128)(2,1)} %copy-done.5) | copy-start | bytes 1179652
  116.3 65.2 %all-to-all-start.1 = ((bf16[64,16,2048]{2,1,0:T(8,128)(2,1)}), bf16[64,16,2048]{2,1,0:T(8,128)(2,1)}, u32[]{:S(2)}, u32[]{:S(2)}) async-start(bf16[64,16,2048]{2,1,0:T(8,128)(2,1)} %get-tuple-element.36), calls=%async_computation.1 | async-start | bytes 8388608 | tf_op jit(solution)/shard_map/all_to_all | solution.py:308
  124.3 6.5 %copy-start.7 = (bf16[512,2048]{1,0:T(8,128)(2,1)S(1)}, bf16[512,2048]{1,0:T(8,128)(2,1)}, u32[]{:S(2)}) copy-start(bf16[512,2048]{1,0:T(8,128)(2,1)} %get-tuple-element.61) | copy-start | bytes 6291460
  124.4 6.5 %copy-start.11 = (bf16[512,768]{1,0:T(8,128)(2,1)S(1)}, bf16[512,768]{1,0:T(8,128)(2,1)}, u32[]{:S(2)}) copy-start(bf16[512,768]{1,0:T(8,128)(2,1)} %get-tuple-element.50) | copy-start | bytes 2359300
  130.6 13.9 %collective-permute-start = (bf16[2048,768]{1,0:T(8,128)(2,1)}, bf16[2048,768]{1,0:T(8,128)(2,1)}, u32[]{:S(2)}, u32[]{:S(2)}) collective-permute-start(bf16[2048,768]{1,0:T(8,128)(2,1)} %convolution_convert_fusion.2), channel_id=1, source_target_pairs={{0,64},{64,0},{1,65},{65,1},{2,66},{66,2},{3,67},{67,3},{4,68},{68... | collective-permute-start | bytes 9437192 | tf_op jit(solution)/shard_map/ppermute | solution.py:312
  130.8 4.4 %copy-start.9 = (s32[128,4]{0,1:T(4,128)S(1)}, s32[128,4]{0,1:T(4,128)}, u32[]{:S(2)}) copy-start(s32[128,4]{0,1:T(4,128)} %param.8) | copy-start | bytes 6148
  130.8 5.1 %copy-start.10 = (f32[128,4]{0,1:T(4,128)S(1)}, f32[128,4]{0,1:T(4,128)}, u32[]{:S(2)}) copy-start(f32[128,4]{0,1:T(4,128)} %param.9) | copy-start | bytes 6148
  134.9 56.9 %collective-permute-start.2 = (bf16[768,2048]{1,0:T(8,128)(2,1)}, bf16[768,2048]{1,0:T(8,128)(2,1)}, u32[]{:S(2)}, u32[]{:S(2)}) collective-permute-start(bf16[768,2048]{1,0:T(8,128)(2,1)} %convolution_convert_fusion), channel_id=1, source_target_pairs={{0,64},{64,0},{1,65},{65,1},{2,66},{66,2},{3,67},{67,3},{4,68},{68... | collective-permute-start | bytes 9437192 | tf_op jit(solution)/shard_map/ppermute | solution.py:312
  181.5 37.3 %all-to-all-start.3 = ((bf16[64,8,2048]{2,1,0:T(8,128)(2,1)}), bf16[64,8,2048]{2,1,0:T(8,128)(2,1)S(1)}, u32[]{:S(2)}, u32[]{:S(2)}) async-start(bf16[64,8,2048]{2,1,0:T(8,128)(2,1)} %get-tuple-element.47), calls=%async_computation.3 | async-start | bytes 4194304 | tf_op jit(solution)/shard_map/all_to_all | solution.py:308
  191.8 6.2 %copy-start.1 = (bf16[384,1024]{1,0:T(8,128)(2,1)S(1)}, bf16[384,1024]{1,0:T(8,128)(2,1)}, u32[]{:S(2)}) copy-start(bf16[384,1024]{1,0:T(8,128)(2,1)} %get-tuple-element.48.pick_ref) | copy-start | bytes 2359300
  198.0 20.7 %copy-start.2 = (bf16[384,512]{1,0:T(8,128)(2,1)S(1)}, bf16[384,512]{1,0:T(8,128)(2,1)}, u32[]{:S(2)}) copy-start(bf16[384,512]{1,0:T(8,128)(2,1)} %get-tuple-element.46.refs_0_) | copy-start | bytes 1179652
  202.0 1.0 copy-start
